TPU v7x, 512 devices: a whole 4x8x8 slice. The times are simulated.
512 devices in a mesh: gx: 32 (over z, y_lo), gy: 16 (over x, y_hi, core).
Axes of the slice: x: 4, y: 8 (y_hi: 2, y_lo: 4; y = y_hi * 4 + y_lo), z: 8, core: 2. Of those that a mesh axis runs over, the one named last changes fastest.
Arguments:
- ensemble: float32 [40, 8, 64, 4096], P(None, None, 'gy', 'gx'), may hold values from 0.2 to 2
- courant_x: float32 [2, 64, 4096], P(None, 'gy', 'gx'), may hold values from -0.4 to 0.4
- courant_y: float32 [2, 64, 4096], P(None, 'gy', 'gx'), may hold values from -0.4 to 0.4
- diffusion: float32 [64, 4096], P('gy', 'gx'), may hold values from 0.02 to 0.12
- mixing: float32 [64, 4096], P('gy', 'gx'), may hold values from 0.02 to 0.2
- growth: float32 [2, 64, 4096], P(None, 'gy', 'gx'), may hold values from 0.05 to 0.5
- land_sea: int32 [64, 4096], P('gy', 'gx'), may hold values 0 or 1
- obs_cell: int32 [2, 1024], replicated, may hold values from 0 to 262143, as said below
- obs_value: float32 [2, 1024], replicated, may hold values from 0.2 to 2
- observation_variance: float32 [2, 1024], replicated, may hold values from 0.05 to 0.5
- obs_perturb: float32 [2, 1024, 40], replicated, may hold values from -4 to 4
- radius: int32 [1], replicated, may hold values from 32 to 64
Outputs:
- analysis: float32 [40, 8, 64, 4096], P(None, None, 'gy', 'gx')
Inputs may be any that keep to these rules, and one draw needn't show every extreme that they name: obs_cell[b, k] is row * 4096 + column of the observed cell; with tiles of 4 rows and 128 columns, in each batch no tile holds more than 8 observed cells and some tile holds exactly 8.
All inputs are finite; a program needn't handle non-finite values. No bound on the sum of `land_sea` on one device may be relied on, other than what follows from the above.
Results may differ from a plain program's by a relative error of at most 0.0003.
Values sent between devices are 32-bit elements; how exact they have to be, the bound alone decides.
A program may use at most 64 MiB of HBM per device.

v0:
```python
import jax
import jax.numpy as jnp
from jax import lax
from jax.sharding import PartitionSpec as P

CAP = 8


def padded_2(x, sides, width):
    for axis, dim in sides:
        size, length = (lax.axis_size(axis), x.shape[dim])
        up = [(i, (i + 1) % size) for i in range(size)]
        down = [(j, i) for i, j in up]
        last = lax.slice_in_dim(x, length - width, length, axis=dim)
        initial = lax.slice_in_dim(x, 0, width, axis=dim)
        before = lax.ppermute(last, axis, up)
        after = lax.ppermute(initial, axis, down)
        x = jnp.concatenate([before, x, after], axis=dim)
    return x


def upwind(minus_two, minus_one, center, plus_one, plus_two, courant):
    rising = (2.0 * plus_one + 3.0 * center - 6.0 * minus_one + minus_two) / 6.0
    falling = (-plus_two + 6.0 * plus_one - 3.0 * center - 2.0 * minus_one) / 6.0
    return -(jnp.maximum(courant, 0.0) * rising + jnp.minimum(courant, 0.0) * falling)


def transport(padded, courant_x, courant_y, diffusion):
    row_count = padded.shape[-2] - 4
    columns = padded.shape[-1] - 4

    def offset(row_shift, col_shift):
        return padded[
            ..., 2 + row_shift : 2 + row_shift + row_count, 2 + col_shift : 2 + col_shift + columns
        ]

    center = offset(0, 0)
    along_x = upwind(
        offset(0, -2), offset(0, -1), center, offset(0, 1), offset(0, 2), courant_x[:, None]
    )
    along_y = upwind(
        offset(-2, 0), offset(-1, 0), center, offset(1, 0), offset(2, 0), courant_y[:, None]
    )
    spread = offset(0, 1) + offset(0, -1) + offset(1, 0) + offset(-1, 0) - 4.0 * center
    return (center, along_x + along_y + diffusion * spread)


def tendency(fields, growth, mixing):
    nutrient = fields[..., 0, :, :]
    plankton = fields[..., 1, :, :]
    grazer = fields[..., 2, :, :]
    detritus = fields[..., 3, :, :]
    uptake = growth * jnp.abs(nutrient) / (jnp.abs(nutrient) + 0.5) * plankton
    grazing = 0.3 * grazer * jnp.abs(plankton) / (jnp.abs(plankton) + 0.5)
    biology = jnp.stack(
        [
            -uptake + 0.1 * detritus,
            uptake - grazing - 0.05 * plankton,
            0.3 * grazing - 0.05 * grazer,
            0.7 * grazing + 0.05 * plankton + 0.05 * grazer - 0.1 * detritus,
        ],
        axis=-3,
    )
    upper_level = fields[..., 0, :, :, :]
    lower_level = fields[..., 1, :, :, :]
    vertical = jnp.stack(
        [mixing * (lower_level - upper_level), mixing * (upper_level - lower_level)], axis=-4
    )
    return biology + vertical


def build_slots(
    present_state,
    cells,
    values,
    variances,
    perturbs,
    tile_id,
    tiles_y,
    row_start,
    col_start,
    total_cols,
):
    members = present_state.shape[0]
    tile_rows = present_state.shape[2]
    tile_cols = present_state.shape[3]
    obs_rows = cells // total_cols
    obs_cols = cells % total_cols
    owners = obs_cols // tile_cols * tiles_y + obs_rows // tile_rows
    ownership_mask = owners == tile_id
    slot_rank = jnp.cumsum(ownership_mask.astype(jnp.int32)) - 1
    slot_hot = (slot_rank[None, :] == jnp.arange(CAP, dtype=jnp.int32)[:, None]) & ownership_mask[
        None, :
    ]
    slot_float = slot_hot.astype(jnp.float32)
    local_cell = (obs_rows - row_start) * tile_cols + (obs_cols - col_start)
    slot_cell = jnp.sum(jnp.where(slot_hot, local_cell[None, :], 0), axis=1)
    filled = jnp.sum(slot_float, axis=1)
    cell_hot = (
        (slot_cell[:, None] == jnp.arange(tile_rows * tile_cols, dtype=jnp.int32)[None, :])
        & (filled[:, None] > 0.0)
    ).astype(jnp.float32)
    plankton_field = present_state[:, 1].reshape(members, tile_rows * tile_cols)
    prior_slots = lax.dot_general(
        cell_hot, plankton_field, (((1,), (1,)), ((), ())), precision=lax.Precision.HIGHEST
    )
    slot_value = jnp.dot(slot_float, values, precision=lax.Precision.HIGHEST)
    slot_var = jnp.dot(slot_float, variances, precision=lax.Precision.HIGHEST)
    slot_noise = jnp.dot(slot_float, perturbs, precision=lax.Precision.HIGHEST)
    slot_row = jnp.dot(slot_float, obs_rows.astype(jnp.float32), precision=lax.Precision.HIGHEST)
    slot_col = jnp.dot(slot_float, obs_cols.astype(jnp.float32), precision=lax.Precision.HIGHEST)
    anomaly = prior_slots - jnp.mean(prior_slots, axis=1, keepdims=True)
    spread_var = jnp.sum(anomaly * anomaly, axis=1) / (members - 1)
    obs_scale = filled / ((members - 1) * (spread_var + slot_var + (1.0 - filled)))
    innovation = slot_value[:, None] + jnp.sqrt(slot_var)[:, None] * slot_noise - prior_slots
    record = jnp.concatenate(
        [anomaly, innovation, obs_scale[:, None], slot_row[:, None], slot_col[:, None]], axis=1
    )
    return record[None]


def local(
    ensemble,
    courant_x,
    courant_y,
    diffusion,
    mixing,
    growth,
    land_sea,
    obs_cell,
    obs_value,
    observation_variance,
    obs_perturb,
    radius,
):
    members, fields, tile_rows, tile_cols = ensemble.shape
    levels = courant_x.shape[0]
    tiles_x = lax.axis_size("gx")
    tiles_y = lax.axis_size("gy")
    tile_x = lax.axis_index("gx")
    tile_y = lax.axis_index("gy")
    total_cols = tile_cols * tiles_x
    total_rows = tile_rows * tiles_y
    ocean_mask = land_sea.astype(jnp.float32)
    padded = padded_2(ensemble, (("gx", 3), ("gy", 2)), 2)
    global_row = tile_y * tile_rows + jnp.arange(tile_rows + 4, dtype=jnp.int32) - 2
    inside = (global_row >= 0) & (global_row < total_rows)
    padded = jnp.where(inside[:, None], padded, 0.0)
    padded = padded.reshape(members, levels, fields // levels, tile_rows + 4, tile_cols + 4)
    center, carried = transport(padded, courant_x, courant_y, diffusion)
    present_state = center + ocean_mask * (carried + tendency(center, growth, mixing))
    present_state = present_state.reshape(members, fields, tile_rows, tile_cols)
    tile_id = tile_x * tiles_y + tile_y
    row_start = tile_y * tile_rows
    col_start = tile_x * tile_cols
    grid_cell_count = tile_rows * tile_cols
    cell_rowf = (
        jnp.broadcast_to(
            (row_start + jnp.arange(tile_rows, dtype=jnp.int32))[:, None], (tile_rows, tile_cols)
        )
        .reshape(grid_cell_count)
        .astype(jnp.float32)
    )
    cell_colf = (
        jnp.broadcast_to(
            (col_start + jnp.arange(tile_cols, dtype=jnp.int32))[None, :], (tile_rows, tile_cols)
        )
        .reshape(grid_cell_count)
        .astype(jnp.float32)
    )
    radius_sq = radius[0].astype(jnp.float32) * radius[0].astype(jnp.float32)
    half_cols = total_cols // 2
    for batch_index in range(obs_value.shape[0]):
        record = build_slots(
            present_state,
            obs_cell[batch_index],
            obs_value[batch_index],
            observation_variance[batch_index],
            obs_perturb[batch_index],
            tile_id,
            tiles_y,
            row_start,
            col_start,
            total_cols,
        )
        column_slots = lax.all_gather(record, "gy", axis=1, tiled=True)
        nearby = padded_2(column_slots, (("gx", 0),), 1)
        member_deviation = (present_state - jnp.mean(present_state, axis=0, keepdims=True)).reshape(
            members, fields * grid_cell_count
        )
        increment = jnp.zeros((members, fields * grid_cell_count), jnp.float32)
        for column_index in range(3):
            slot_block = nearby[column_index]
            block_size = slot_block.shape[0]
            slot_anom = slot_block[:, :members]
            slot_innov = slot_block[:, members : 2 * members]
            obs_scale = slot_block[:, 2 * members]
            slot_row = slot_block[:, 2 * members + 1]
            slot_col = slot_block[:, 2 * members + 2]
            col_gap = (
                jnp.mod(slot_col[:, None] - cell_colf[None, :] + half_cols, total_cols) - half_cols
            )
            row_gap = slot_row[:, None] - cell_rowf[None, :]
            taper_weight = jnp.maximum(
                0.0, 1.0 - (row_gap * row_gap + col_gap * col_gap) / radius_sq
            )
            weight = taper_weight * obs_scale[:, None]
            covariance = lax.dot_general(
                slot_anom,
                member_deviation,
                (((1,), (0,)), ((), ())),
                precision=lax.Precision.HIGHEST,
            )
            gain_block = (
                covariance.reshape(block_size, fields, grid_cell_count) * weight[:, None, :]
            ).reshape(block_size, fields * grid_cell_count)
            increment = increment + lax.dot_general(
                slot_innov, gain_block, (((0,), (0,)), ((), ())), precision=lax.Precision.HIGHEST
            )
        present_state = present_state + ocean_mask * increment.reshape(
            members, fields, tile_rows, tile_cols
        )
    return present_state


def solution(mesh):
    placed = (
        P(None, None, "gy", "gx"),
        P(None, "gy", "gx"),
        P(None, "gy", "gx"),
        P("gy", "gx"),
        P("gy", "gx"),
        P(None, "gy", "gx"),
        P("gy", "gx"),
        P(),
        P(),
        P(),
        P(),
        P(),
    )
    return jax.shard_map(
        local, mesh=mesh, in_specs=placed, out_specs=P(None, None, "gy", "gx"), check_vma=False
    )
```

profile of v0, /device:TPU:1, one launch (start us, length us, event | category | flops | bytes accessed | tf_op | source)
XLA Modules:
  0.0 205.8 jit_solution(6187460439538034503)
XLA Ops:
  0.0 1.8 fusion.195
  1.8 0.4 copy.201
  2.2 14.5 %collective-permute-start.1 = (f32[40,8,4,2]{0,1,3,2:T(8,128)S(1)}, f32[40,8,4,2]{0,1,3,2:T(8,128)S(1)}, u32[]{:S(2)}, u32[]{:S(2)}) collective-permute-start(f32[40,8,4,2]{0,1,3,2:T(8,128)S(1)} %copy.201), channel_id=1, source_target_pairs={{16,0},{32,16},{48,32},{64,48},{80,64},{96,80},{112,96},{128,112},... | collective-permute-start | bytes 30728 | tf_op jit(solution)/shard_map/ppermute | solution.py:17
  16.8 0.4 copy.200
  17.2 1.9 collective-permute-start
  19.4 0.3 reduce-window.16
  20.5 0.3 reduce-window.24
  21.3 0.6 select_reduce_fusion
  21.9 0.5 broadcast_compare_fusion
  22.4 0.7 convolution_bitcast_fusion.5
  23.2 0.7 convolution_bitcast_fusion.1
  23.9 0.7 convolution_bitcast_fusion
  25.5 0.6 copy.156
  26.2 0.6 copy.154
  26.8 0.6 pad_maximum_fusion
  27.5 3.6 %collective-permute-start.3 = (f32[40,8,2,132]{3,1,2,0:T(8,128)S(1)}, f32[40,8,2,132]{3,1,2,0:T(8,128)S(1)}, u32[]{:S(2)}, u32[]{:S(2)}) collective-permute-start(f32[40,8,2,132]{3,1,2,0:T(8,128)S(1)} %get-tuple-element.42), channel_id=1, source_target_pairs={{1,0},{2,1},{3,2},{4,3},{5,4},{6,5},{7,6},{8,7},{9,8},{10,9},{11,1... | collective-permute-start | bytes 1013768 | tf_op jit(solution)/shard_map/ppermute | solution.py:17
  31.1 5.8 %collective-permute-start.2 = (f32[40,8,2,132]{3,1,2,0:T(8,128)S(1)}, f32[40,8,2,132]{3,1,2,0:T(8,128)S(1)}, u32[]{:S(2)}, u32[]{:S(2)}) collective-permute-start(f32[40,8,2,132]{3,1,2,0:T(8,128)S(1)} %get-tuple-element.41), channel_id=1, source_target_pairs={{0,1},{1,2},{2,3},{3,4},{4,5},{5,6},{6,7},{7,8},{8,9},{9,10},{10,1... | collective-permute-start | bytes 1013768 | tf_op jit(solution)/shard_map/ppermute | solution.py:16
  37.2 0.8 copy.158
  37.9 21.4 %collective-permute-done.3 = f32[40,8,2,132]{3,1,2,0:T(8,128)S(1)} collective-permute-done((f32[40,8,2,132]{3,1,2,0:T(8,128)S(1)}, f32[40,8,2,132]{3,1,2,0:T(8,128)S(1)}, u32[]{:S(2)}, u32[]{:S(2)}) %collective-permute-start.3) | collective-permute-done | bytes 337952 | tf_op jit(solution)/shard_map/ppermute | solution.py:17
  59.4 0.4 copy.159
  59.8 0.4 copy.157
  60.2 0.3 maximum_select_fusion
  60.5 0.3 copy-done.19
  60.8 0.2 subtract_multiply_fusion.1
  61.1 0.2 negate_add_fusion
  61.5 1.5 fusion.192
  63.1 0.3 fusion.197
  64.1 27.1 %all-gather = f32[128,83]{1,0:T(8,128)S(1)} all-gather(f32[8,83]{1,0:T(8,128)S(1)} %concatenate.24), channel_id=2, replica_groups=mesh['gx'=32,'gy'=16] {'gy'}, dimensions={0}, use_global_device_ids=true | all-gather | bytes 45152 | tf_op jit(solution)/shard_map/all_gather | solution.py:186
  91.2 5.3 %collective-permute-start.4 = (f32[1,128,83]{2,1,0:T(8,128)S(1)}, f32[1,128,83]{2,1,0:T(8,128)S(1)}, u32[]{:S(2)}, u32[]{:S(2)}) collective-permute-start(f32[1,128,83]{2,1,0:T(8,128)S(1)} %bitcast.182), channel_id=1, source_target_pairs={{0,16},{16,32},{32,48},{48,64},{64,80},{80,96},{96,112},{112,128},... | collective-permute-start | bytes 127496 | tf_op jit(solution)/shard_map/ppermute | solution.py:16
  96.6 7.9 %collective-permute-start.5 = (f32[1,128,83]{2,1,0:T(8,128)S(1)}, f32[1,128,83]{2,1,0:T(8,128)S(1)}, u32[]{:S(2)}, u32[]{:S(2)}) collective-permute-start(f32[1,128,83]{2,1,0:T(8,128)S(1)} %bitcast.183), channel_id=1, source_target_pairs={{16,0},{32,16},{48,32},{64,48},{80,64},{96,80},{112,96},{128,112},... | collective-permute-start | bytes 127496 | tf_op jit(solution)/shard_map/ppermute | solution.py:17
  104.6 0.3 reshape.696
  105.0 0.2 slice_reduce_fusion.14
  105.2 0.2 slice_reduce_fusion.17
  105.8 1.5 fusion.95
  107.3 3.1 %convolution_multiply_fusion.3 = f32[128,8,512]{2,0,1:T(8,128)} fusion(f32[128,512]{1,0:T(8,128)S(1)} %get-tuple-element.57, f32[5,8,8,512]{3,2,1,0:T(8,128)S(1)} %bitcast.166, f32[128,83]{1,0:T(8,128)S(1)} %bitcast.194), kind=kOutput, calls=%fused_computation.8 | convolution fusion | flops 252182528 | bytes 3057152 | tf_op jit(solution)/shard_map/dot_general | solution.py:208
  110.5 1.9 copy.173
  112.4 4.0 %fusion.117 = f32[40,4096]{1,0:T(8,128)} fusion(f32[128,4096]{0,1:T(8,128)S(1)} %bitcast.171, f32[128,83]{1,0:T(8,128)} %bitcast.195), kind=kOutput, calls=%fused_computation.187 | convolution fusion | flops 251658240 | bytes 2795008 | tf_op jit(solution)/shard_map/dot_general | solution.py:217
  116.4 3.1 %convolution_multiply_fusion.4 = f32[128,8,512]{2,0,1:T(8,128)} fusion(f32[128,512]{1,0:T(8,128)S(1)} %copy-done.8, f32[5,8,8,512]{3,2,1,0:T(8,128)S(1)} %bitcast.167, f32[128,83]{1,0:T(8,128)S(1)} %all-gather), kind=kOutput, calls=%fused_computation.9 | convolution fusion | flops 252182528 | bytes 3057152 | tf_op jit(solution)/shard_map/dot_general | solution.py:208
  119.6 1.9 copy.170
  121.5 3.2 %fusion.119 = f32[40,4096]{1,0:T(8,128)} fusion(f32[128,4096]{0,1:T(8,128)S(1)} %bitcast.172, f32[128,83]{1,0:T(8,128)S(1)} %all-gather), kind=kOutput, calls=%fused_computation.193 | convolution fusion | flops 251658240 | bytes 2795008 | tf_op jit(solution)/shard_map/dot_general | solution.py:217
  124.7 3.1 %convolution_multiply_fusion.5 = f32[128,8,512]{2,0,1:T(8,128)} fusion(f32[128,512]{1,0:T(8,128)S(1)} %copy-done.6, f32[5,8,8,512]{3,2,1,0:T(8,128)S(1)} %bitcast.168, f32[128,83]{1,0:T(8,128)S(1)} %bitcast.188), kind=kOutput, calls=%fused_computation.10 | convolution fusion | flops 252182528 | bytes 3057152 | tf_op jit(solution)/shard_map/dot_general | solution.py:208
  127.8 1.9 copy.167
  129.7 3.6 %fusion.1 = f32[40,4096]{1,0:T(8,128)S(1)} fusion(f32[40,4096]{1,0:T(8,128)} %fusion.117, f32[40,4096]{1,0:T(8,128)} %fusion.119, f32[128,4096]{0,1:T(8,128)S(1)} %bitcast.169, f32[128,83]{1,0:T(8,128)S(1)} %bitcast.189), kind=kOutput, calls=%fused_computation.3 | convolution fusion | flops 251985920 | bytes 4105728 | tf_op jit(solution)/shard_map/dot_general | solution.py:217
  133.4 0.4 reshape.700
  133.9 0.2 copy_add_fusion
  134.2 0.3 fusion.198
  135.3 29.8 %all-gather.1 = f32[128,83]{1,0:T(8,128)S(1)} all-gather(f32[8,83]{1,0:T(8,128)S(1)} %concatenate.25), channel_id=3, replica_groups=mesh['gx'=32,'gy'=16] {'gy'}, dimensions={0}, use_global_device_ids=true | all-gather | bytes 45152 | tf_op jit(solution)/shard_map/all_gather | solution.py:186
  165.0 1.9 collective-permute-start.6
  167.0 8.2 %collective-permute-start.7 = (f32[1,128,83]{2,1,0:T(8,128)S(1)}, f32[1,128,83]{2,1,0:T(8,128)S(1)}, u32[]{:S(2)}, u32[]{:S(2)}) collective-permute-start(f32[1,128,83]{2,1,0:T(8,128)S(1)} %bitcast.181), channel_id=1, source_target_pairs={{16,0},{32,16},{48,32},{64,48},{80,64},{96,80},{112,96},{128,112},... | collective-permute-start | bytes 127496 | tf_op jit(solution)/shard_map/ppermute | solution.py:17
  175.2 0.4 reshape.702
  175.6 0.4 fusion.35
  176.4 0.2 slice_reduce_fusion.8
  176.9 1.5 fusion.86
  178.4 3.1 %convolution_multiply_fusion = f32[128,8,512]{2,0,1:T(8,128)} fusion(f32[128,512]{1,0:T(8,128)S(1)} %get-tuple-element.52, f32[5,8,8,512]{3,2,1,0:T(8,128)S(1)} %bitcast.163, f32[128,83]{1,0:T(8,128)S(1)} %bitcast.191), kind=kOutput, calls=%fused_computation.5 | convolution fusion | flops 252182528 | bytes 3057152 | tf_op jit(solution)/shard_map/dot_general | solution.py:208
  181.5 1.9 copy.187
  183.4 4.0 %fusion.112 = f32[40,4096]{1,0:T(8,128)} fusion(f32[128,4096]{0,1:T(8,128)S(1)} %bitcast.173, f32[128,83]{1,0:T(8,128)} %bitcast.192), kind=kOutput, calls=%fused_computation.170 | convolution fusion | flops 251658240 | bytes 2795008 | tf_op jit(solution)/shard_map/dot_general | solution.py:217
  187.5 3.1 %convolution_multiply_fusion.1 = f32[128,8,512]{2,0,1:T(8,128)} fusion(f32[128,512]{1,0:T(8,128)S(1)} %copy-done.7, f32[5,8,8,512]{3,2,1,0:T(8,128)S(1)} %bitcast.164, f32[128,83]{1,0:T(8,128)S(1)} %all-gather.1), kind=kOutput, calls=%fused_computation.6 | convolution fusion | flops 252182528 | bytes 3057152 | tf_op jit(solution)/shard_map/dot_general | solution.py:208
  190.6 1.9 copy.184
  192.5 3.2 %fusion.114 = f32[40,4096]{1,0:T(8,128)} fusion(f32[128,4096]{0,1:T(8,128)S(1)} %bitcast.174, f32[128,83]{1,0:T(8,128)S(1)} %all-gather.1), kind=kOutput, calls=%fused_computation.176 | convolution fusion | flops 251658240 | bytes 2795008 | tf_op jit(solution)/shard_map/dot_general | solution.py:217
  195.7 3.1 %convolution_multiply_fusion.2 = f32[128,8,512]{2,0,1:T(8,128)} fusion(f32[128,512]{1,0:T(8,128)S(1)} %copy-done.5, f32[5,8,8,512]{3,2,1,0:T(8,128)S(1)} %bitcast.165, f32[128,83]{1,0:T(8,128)S(1)} %bitcast.185), kind=kOutput, calls=%fused_computation.7 | convolution fusion | flops 252182528 | bytes 3057152 | tf_op jit(solution)/shard_map/dot_general | solution.py:208
  198.8 1.9 copy.181
  200.7 3.6 %fusion = f32[40,4096]{1,0:T(8,128)S(1)} fusion(f32[40,4096]{1,0:T(8,128)} %fusion.112, f32[40,4096]{1,0:T(8,128)} %fusion.114, f32[128,4096]{0,1:T(8,128)S(1)} %bitcast.170, f32[128,83]{1,0:T(8,128)S(1)} %bitcast.186), kind=kOutput, calls=%fused_computation.1 | convolution fusion | flops 251985920 | bytes 4105728 | tf_op jit(solution)/shard_map/dot_general | solution.py:217
  204.3 0.4 reshape.706
  204.8 1.0 multiply_add_fusion.2
  (121 shorter events, 4.8 us)
Async XLA Ops:
  0.0 24.8 %copy-start = (f32[40,8,4,128]{3,2,1,0:T(4,128)S(1)}, f32[40,8,4,128]{3,2,1,0:T(4,128)}, u32[]{:S(2)}) copy-start(f32[40,8,4,128]{3,2,1,0:T(4,128)} %param.12) | copy-start | bytes 1966084
  0.0 19.1 %copy-start.11 = (s32[2,1024]{1,0:T(2,128)S(1)}, s32[2,1024]{1,0:T(2,128)}, u32[]{:S(2)}) copy-start(s32[2,1024]{1,0:T(2,128)} %param.19) | copy-start | bytes 24580
  0.0 22.4 %copy-start.26 = (f32[2,1024]{1,0:T(2,128)S(1)}, f32[2,1024]{1,0:T(2,128)}, u32[]{:S(2)}) copy-start(f32[2,1024]{1,0:T(2,128)} %param.20) | copy-start | bytes 24580
  1.8 23.0 %copy-start.21 = (s32[4,128]{1,0:T(4,128)S(1)}, s32[4,128]{1,0:T(4,128)}, u32[]{:S(2)}) copy-start(s32[4,128]{1,0:T(4,128)} %param.18) | copy-start | bytes 6148
  2.2 23.3 %collective-permute-start.1 = (f32[40,8,4,2]{0,1,3,2:T(8,128)S(1)}, f32[40,8,4,2]{0,1,3,2:T(8,128)S(1)}, u32[]{:S(2)}, u32[]{:S(2)}) collective-permute-start(f32[40,8,4,2]{0,1,3,2:T(8,128)S(1)} %copy.201), channel_id=1, source_target_pairs={{16,0},{32,16},{48,32},{64,48},{80,64},{96,80},{112,96},{128,112},... | collective-permute-start | bytes 30728 | tf_op jit(solution)/shard_map/ppermute | solution.py:17
  17.2 8.9 %collective-permute-start = (f32[40,8,4,2]{0,1,3,2:T(8,128)S(1)}, f32[40,8,4,2]{0,1,3,2:T(8,128)S(1)}, u32[]{:S(2)}, u32[]{:S(2)}) collective-permute-start(f32[40,8,4,2]{0,1,3,2:T(8,128)S(1)} %copy.200), channel_id=1, source_target_pairs={{0,16},{16,32},{32,48},{48,64},{64,80},{80,96},{96,112},{112,128},... | collective-permute-start | bytes 30728 | tf_op jit(solution)/shard_map/ppermute | solution.py:16
  19.3 6.8 %copy-start.12 = (pred[1024]{0:T(1024)(128)(4,1)}, pred[1024]{0:T(1024)(128)(4,1)S(1)}, u32[]{:S(2)}) copy-start(pred[1024]{0:T(1024)(128)(4,1)S(1)} %get-tuple-element.25) | copy-start | bytes 3076
  21.3 1.9 copy-start.24
  27.4 9.7 %copy-start.15 = (f32[2,4,128]{2,1,0:T(4,128)S(1)}, f32[2,4,128]{2,1,0:T(4,128)}, u32[]{:S(2)}) copy-start(f32[2,4,128]{2,1,0:T(4,128)} %param.14) | copy-start | bytes 12292
  27.4 9.7 %copy-start.16 = (f32[2,4,128]{2,1,0:T(4,128)S(1)}, f32[2,4,128]{2,1,0:T(4,128)}, u32[]{:S(2)}) copy-start(f32[2,4,128]{2,1,0:T(4,128)} %param.13) | copy-start | bytes 12292
  27.5 31.9 %collective-permute-start.3 = (f32[40,8,2,132]{3,1,2,0:T(8,128)S(1)}, f32[40,8,2,132]{3,1,2,0:T(8,128)S(1)}, u32[]{:S(2)}, u32[]{:S(2)}) collective-permute-start(f32[40,8,2,132]{3,1,2,0:T(8,128)S(1)} %get-tuple-element.42), channel_id=1, source_target_pairs={{1,0},{2,1},{3,2},{4,3},{5,4},{6,5},{7,6},{8,7},{9,8},{10,9},{11,1... | collective-permute-start | bytes 1013768 | tf_op jit(solution)/shard_map/ppermute | solution.py:17
  31.1 28.6 %collective-permute-start.2 = (f32[40,8,2,132]{3,1,2,0:T(8,128)S(1)}, f32[40,8,2,132]{3,1,2,0:T(8,128)S(1)}, u32[]{:S(2)}, u32[]{:S(2)}) collective-permute-start(f32[40,8,2,132]{3,1,2,0:T(8,128)S(1)} %get-tuple-element.41), channel_id=1, source_target_pairs={{0,1},{1,2},{2,3},{3,4},{4,5},{5,6},{6,7},{7,8},{8,9},{9,10},{10,1... | collective-permute-start | bytes 1013768 | tf_op jit(solution)/shard_map/ppermute | solution.py:16
  60.2 0.7 copy-start.19
  60.2 0.9 copy-start.14
  60.8 0.7 copy-start.20
  61.5 2.0 copy-start.27
  61.5 2.3 %copy-start.9 = (f32[2,1024,40]{1,2,0:T(8,128)S(1)}, f32[2,1024,40]{1,2,0:T(8,128)}, u32[]{:S(2)}) copy-start(f32[2,1024,40]{1,2,0:T(8,128)} %param.22) | copy-start | bytes 983044
  91.2 14.0 %collective-permute-start.4 = (f32[1,128,83]{2,1,0:T(8,128)S(1)}, f32[1,128,83]{2,1,0:T(8,128)S(1)}, u32[]{:S(2)}, u32[]{:S(2)}) collective-permute-start(f32[1,128,83]{2,1,0:T(8,128)S(1)} %bitcast.182), channel_id=1, source_target_pairs={{0,16},{16,32},{32,48},{48,64},{64,80},{80,96},{96,112},{112,128},... | collective-permute-start | bytes 127496 | tf_op jit(solution)/shard_map/ppermute | solution.py:16
  96.6 9.0 %collective-permute-start.5 = (f32[1,128,83]{2,1,0:T(8,128)S(1)}, f32[1,128,83]{2,1,0:T(8,128)S(1)}, u32[]{:S(2)}, u32[]{:S(2)}) collective-permute-start(f32[1,128,83]{2,1,0:T(8,128)S(1)} %bitcast.183), channel_id=1, source_target_pairs={{16,0},{32,16},{48,32},{64,48},{80,64},{96,80},{112,96},{128,112},... | collective-permute-start | bytes 127496 | tf_op jit(solution)/shard_map/ppermute | solution.py:17
  104.9 2.4 %copy-start.1 = (f32[40,4096]{1,0:T(8,128)}, f32[40,4096]{1,0:T(8,128)S(1)}, u32[]{:S(2)}) copy-start(f32[40,4096]{1,0:T(8,128)S(1)} %reshape.696) | copy-start | bytes 1966084
  105.6 1.8 copy-start.4
  112.4 4.0 %copy-start.8 = (f32[128,512]{1,0:T(8,128)S(1)}, f32[128,512]{1,0:T(8,128)}, u32[]{:S(2)}) copy-start(f32[128,512]{1,0:T(8,128)} %get-tuple-element.56) | copy-start | bytes 786436
  121.5 3.2 %copy-start.6 = (f32[128,512]{1,0:T(8,128)S(1)}, f32[128,512]{1,0:T(8,128)}, u32[]{:S(2)}) copy-start(f32[128,512]{1,0:T(8,128)} %get-tuple-element.55) | copy-start | bytes 786436
  133.3 0.8 copy-start.23
  133.3 0.8 copy-start.29
  133.3 1.3 copy-start.13
  133.3 1.3 copy-start.25
  133.4 1.3 copy-start.28
  133.4 1.6 copy-start.10
  133.4 1.6 copy-start.22
  133.4 1.7 copy-start.17
  133.4 1.8 copy-start.18
  134.1 42.0 %copy-start.2 = (f32[40,4096]{1,0:T(8,128)S(1)}, f32[40,4096]{1,0:T(8,128)}, u32[]{:S(2)}) copy-start(f32[40,4096]{1,0:T(8,128)} %copy-done.1) | copy-start | bytes 1966084
  165.0 11.3 %collective-permute-start.6 = (f32[1,128,83]{2,1,0:T(8,128)S(1)}, f32[1,128,83]{2,1,0:T(8,128)S(1)}, u32[]{:S(2)}, u32[]{:S(2)}) collective-permute-start(f32[1,128,83]{2,1,0:T(8,128)S(1)} %bitcast.180), channel_id=1, source_target_pairs={{0,16},{16,32},{32,48},{48,64},{64,80},{80,96},{96,112},{112,128},... | collective-permute-start | bytes 127496 | tf_op jit(solution)/shard_map/ppermute | solution.py:16
  167.0 9.7 %collective-permute-start.7 = (f32[1,128,83]{2,1,0:T(8,128)S(1)}, f32[1,128,83]{2,1,0:T(8,128)S(1)}, u32[]{:S(2)}, u32[]{:S(2)}) collective-permute-start(f32[1,128,83]{2,1,0:T(8,128)S(1)} %bitcast.181), channel_id=1, source_target_pairs={{16,0},{32,16},{48,32},{64,48},{80,64},{96,80},{112,96},{128,112},... | collective-permute-start | bytes 127496 | tf_op jit(solution)/shard_map/ppermute | solution.py:17
  176.6 1.8 copy-start.3
  183.4 4.0 %copy-start.7 = (f32[128,512]{1,0:T(8,128)S(1)}, f32[128,512]{1,0:T(8,128)}, u32[]{:S(2)}) copy-start(f32[128,512]{1,0:T(8,128)} %get-tuple-element.51) | copy-start | bytes 786436
  192.5 3.2 %copy-start.5 = (f32[128,512]{1,0:T(8,128)S(1)}, f32[128,512]{1,0:T(8,128)}, u32[]{:S(2)}) copy-start(f32[128,512]{1,0:T(8,128)} %get-tuple-element.50) | copy-start | bytes 786436
where the time goes:
time: 206 us
  blocking collectives  56.9 us (28%)
  starting transfers between devices  49.2 us (24%)
  matrix products  44.2 us (21%)
  local copies, waits for them, and re-layouts  21.7 us (11%)
  waiting for transfers between devices  21.6 us (10%)
  other arithmetic  10.6 us (5%)
    all_gather x2, blocking collectives, local(): column_slots = lax.all_gather(record, 'gy', axis=1, tiled=True)  56.9 us
    ppermute x4, starting transfers between devices, padded_2(): after = lax.ppermute(initial, axis, down)  34.2 us
    dot_general x6, matrix products, local(): lax.dot_general(slot_innov, gain_block, (((0,), (0,)), ((), ())), precisi...  21.6 us
    ppermute x4, waiting for transfers between devices, padded_2(): after = lax.ppermute(initial, axis, down)  21.6 us
    dot_general x6, matrix products, local(): lax.dot_general(slot_anom, member_deviation, (((1,), (0,)), ((), ())), pr...  18.8 us
    ppermute x4, starting transfers between devices, padded_2(): before = lax.ppermute(last, axis, up)  15 us
    mul x6, local copies, waits for them, and re-layouts, local(): covariance.reshape(block_size, fields, grid_cell_count) * weight[:, None, :]  11.4 us
  transfers between devices with their start and end apart: 8, of which 2 were waited for; matrix products, arithmetic and copies ran while one was open for 5% of the time, Pallas kernels for 0%

commit v1 on v0

v1 whole, which is shorter than its diff:
```python
import functools

import jax
import jax.numpy as jnp
from jax import lax
from jax.experimental import pallas as pl
from jax.experimental.pallas import tpu as pltpu
from jax.sharding import PartitionSpec as P

MESH = pl.DeviceIdType.MESH
F32 = jnp.float32
BF16 = jnp.bfloat16
M = 40
FIELDS = 8
ROWS = 4
COLS = 128
TX = 32
TY = 16
NX = 4096
NOBS = 1024
CAP = 8
SLOTS = 3 * TY * CAP
CHUNKS = NOBS // 128
BLOCK = 128
ORDER = (1, 0, 2, 3, 4, 5, 6, 7)
PARTNERS = [
    (dc, dj) for dj in (4, 3, 5, 2, 6, 1, 7, 0) for dc in (1, -1, 0) if (dc, dj) != (0, 0)
]


def dot(a, b):
    return lax.dot_general(a, b, (((1,), (0,)), ((), ())), preferred_element_type=F32)


def dot_t(a, b):
    return lax.dot_general(a, b, (((1,), (1,)), ((), ())), preferred_element_type=F32)


def split3(x):
    high = x.astype(BF16)
    rest = x - high.astype(F32)
    mid = rest.astype(BF16)
    low = (rest - mid.astype(F32)).astype(BF16)
    return high, mid, low


def iota(shape, dim):
    return lax.broadcasted_iota(jnp.int32, shape, dim)


def forecast_kernel(
    ens_ref,
    cx_ref,
    cy_ref,
    diff_ref,
    mix_ref,
    growth_ref,
    land_ref,
    cell_ref,
    value_ref,
    var_ref,
    pert_ref,
    radius_ref,
    x_ref,
    slots_ref,
    tab_ref,
    row_ref,
    count_ref,
    y_ref,
    halo_ref,
    edge_ref,
    side_ref,
    rec_ref,
    got_ref,
    cell_s,
    rank_s,
    trans_s,
    v_ref,
    hot_ref,
    coef_ref,
    load_sem,
    halo_send,
    halo_recv,
    edge_send,
    edge_recv,
    rec_send,
    rec_recv,
    swap_send,
    swap_recv,
):
    gx = lax.axis_index("gx")
    gy = lax.axis_index("gy")
    core = lax.rem(gy, 2)
    above = (gx, lax.rem(gy + TY - 1, TY))
    below = (gx, lax.rem(gy + 1, TY))
    left = (lax.rem(gx + TX - 1, TX), gy)
    right = (lax.rem(gx + 1, TX), gy)
    sibling = (gx, gy + 1 - 2 * core)

    def partner(dc, dj):
        return (lax.rem(gx + dc + TX, TX), lax.rem(gy + 2 * dj, TY))

    barrier = pltpu.get_barrier_semaphore()
    for device in [partner(dc, dj) for dc, dj in PARTNERS] + [above, below]:
        pl.semaphore_signal(barrier, inc=1, device_id=device, device_id_type=MESH)

    loads = []
    for f in ORDER:
        for r in range(ROWS):
            copy = pltpu.make_async_copy(
                ens_ref.at[:, f * ROWS + r, 0, :], y_ref.at[f, r], load_sem.at[f, r]
            )
            copy.start()
            loads.append(copy)

    col_start = gx * COLS
    row_start = gy * ROWS
    me = gx * TY + gy
    sub = iota((8, 128), 0)
    lane = iota((8, 128), 1)
    big_sub = iota((128, 128), 0)
    big_lane = iota((128, 128), 1)
    own_hot = []
    places = []
    for b in range(2):
        for j in range(CHUNKS):
            cell_s[b, j : j + 1, :] = cell_ref[b : b + 1, 128 * j : 128 * j + 128]
        cell = cell_s[b]
        row = cell >> 12
        col = cell & (NX - 1)
        tile_col = col >> 7
        owner = (tile_col * TY + (row >> 2)).astype(F32)
        for i in range(CHUNKS):
            trans_s[i] = jnp.broadcast_to(owner[i : i + 1, :], (128, 128)).T
        for j in range(CHUNKS):
            mine = jnp.broadcast_to(owner[j : j + 1, :], (128, 128))
            total = jnp.where((trans_s[j] == mine) & (big_sub < big_lane), 1.0, 0.0)
            for i in range(j):
                total = total + jnp.where(trans_s[i] == mine, 1.0, 0.0)
            rank_s[b, j : j + 1, :] = jnp.sum(total, axis=0, keepdims=True)
        rank = rank_s[b]
        own_slot = jnp.where(owner == me.astype(F32), rank, -1.0)
        local_cell = ((row - row_start) * COLS + (col - col_start)).astype(F32)
        subf = sub.astype(F32)
        spot = jnp.zeros((8, 128), F32)
        fill = jnp.zeros((8, 128), F32)
        for j in range(CHUNKS):
            hit = subf == own_slot[j : j + 1, :]
            spot = spot + jnp.where(hit, local_cell[j : j + 1, :], 0.0)
            fill = fill + jnp.where(hit, 1.0, 0.0)
        spot = jnp.sum(spot, axis=1, keepdims=True)
        fill = jnp.sum(fill, axis=1, keepdims=True)
        lane512 = iota((8, ROWS * COLS), 1).astype(F32)
        own_hot.append(jnp.where((spot == lane512) & (fill > 0.0), 1.0, 0.0))
        places.append((row, col, tile_col, rank))
    own_hot = jnp.concatenate(own_hot, axis=0).astype(BF16)

    ocean = land_ref[...].astype(F32)
    first = gy == 0
    last = gy == TY - 1
    for level in range(2):
        for r in range(ROWS):
            at = level * ROWS + r
            o = ocean[r : r + 1, :]
            d = diff_ref[r : r + 1, :] * o
            cx = cx_ref[at : at + 1, :] * o
            cy = cy_ref[at : at + 1, :] * o
            xp, xn = jnp.maximum(cx, 0.0), jnp.minimum(cx, 0.0)
            yp, yn = jnp.maximum(cy, 0.0), jnp.minimum(cy, 0.0)
            terms = [
                1.0 + 0.5 * (xn - xp + yn - yp) - 4.0 * d,
                xn / 6.0,
                d - xp / 3.0 - xn,
                d + xp + xn / 3.0,
                -xp / 6.0,
                yn / 6.0,
                d - yp / 3.0 - yn,
                d + yp + yn / 3.0,
                -yp / 6.0,
            ]
            if r == 0:
                terms[7] = jnp.where(first, 0.0, terms[7])
            if r <= 1:
                terms[8] = jnp.where(first, 0.0, terms[8])
            if r == 3:
                terms[6] = jnp.where(last, 0.0, terms[6])
            if r >= 2:
                terms[5] = jnp.where(last, 0.0, terms[5])
            for i, term in enumerate(terms):
                coef_ref[at, i] = jnp.broadcast_to(term, (8, 128))
            coef_ref[at, 9] = jnp.broadcast_to(o * mix_ref[r : r + 1, :], (8, 128))
            coef_ref[at, 10] = jnp.broadcast_to(o, (8, 128))
            coef_ref[at, 11] = jnp.broadcast_to(growth_ref[at : at + 1, :], (8, 128))

    for n, f in enumerate(ORDER):
        for r in range(ROWS):
            loads[n * ROWS + r].wait()
        packed = jnp.zeros((8, 128), F32)
        for r in range(ROWS):
            for i in range(M // 8):
                at = 4 * (r * (M // 8) + i)
                moved = pltpu.roll(y_ref[f, r, 8 * i : 8 * i + 8, :], (at + 2) % 128, 1)
                packed = jnp.where((lane >= at) & (lane < at + 4), moved, packed)
        edge_ref[n] = packed

    pl.semaphore_wait(barrier, len(PARTNERS) + 2)

    halos = {}

    def send_rows(f):
        for side, (device, start) in enumerate(((below, 2), (above, 0))):
            copy = pltpu.make_async_remote_copy(
                src_ref=y_ref.at[f, pl.ds(start, 2)],
                dst_ref=halo_ref.at[f, side],
                send_sem=halo_send.at[f, side],
                recv_sem=halo_recv.at[f, side],
                device_id=device,
                device_id_type=MESH,
            )
            copy.start()
            halos[f, side] = copy

    edges = {}

    def send_edges(part, window):
        for side, device in enumerate((right, left)):
            copy = pltpu.make_async_remote_copy(
                src_ref=edge_ref.at[window],
                dst_ref=side_ref.at[side, window],
                send_sem=edge_send.at[part, side],
                recv_sem=edge_recv.at[part, side],
                device_id=device,
                device_id_type=MESH,
            )
            copy.start()
            edges[part, side] = copy

    send_rows(ORDER[0])
    send_edges(0, pl.ds(0, 1))
    send_edges(1, pl.ds(1, FIELDS - 1))
    for f in ORDER[1:]:
        send_rows(f)

    def by_member(value, r, at):
        return jnp.broadcast_to(coef_ref[at, value][None], (M // 8, 8, 128)).reshape(M, 128)

    wide_lane = iota((M, 128), 1)

    def inner(n, f):
        level, tracer = divmod(f, 4)
        base = level * 4
        merged = jnp.where((lane & 3) < 2, side_ref[0, n], side_ref[1, n])
        for r in range(ROWS):
            at = level * ROWS + r
            c = functools.partial(by_member, r=r, at=at)
            q = y_ref[f, r]
            halo = jnp.concatenate(
                [
                    pltpu.roll(merged, (126 - 4 * (r * (M // 8) + i)) % 128, 1)
                    for i in range(M // 8)
                ],
                axis=0,
            )
            total = q * c(0)
            total += c(1) * pltpu.roll(jnp.where(wide_lane < 2, halo, q), 126, 1)
            total += c(2) * pltpu.roll(jnp.where(wide_lane < 1, halo, q), 127, 1)
            total += c(3) * pltpu.roll(jnp.where(wide_lane > 126, halo, q), 1, 1)
            total += c(4) * pltpu.roll(jnp.where(wide_lane > 125, halo, q), 2, 1)
            for value, shift in ((5, 2), (6, 1), (7, -1), (8, -2)):
                if 0 <= r + shift < ROWS:
                    total += c(value) * y_ref[f, r + shift]
            total += c(9) * (y_ref[(1 - level) * 4 + tracer, r] - q)
            plankton = y_ref[base + 1, r]
            grazer = y_ref[base + 2, r]
            uptake = grazing = 0.0
            if tracer in (0, 1):
                nutrient = jnp.abs(y_ref[base, r])
                uptake = c(11) * nutrient / (nutrient + 0.5) * plankton
            if tracer in (1, 2, 3):
                size = jnp.abs(plankton)
                grazing = 0.3 * grazer * size / (size + 0.5)
            if tracer == 0:
                change = 0.1 * y_ref[base + 3, r] - uptake
            elif tracer == 1:
                change = uptake - grazing - 0.05 * plankton
            elif tracer == 2:
                change = 0.3 * grazing - 0.05 * grazer
            else:
                change = 0.7 * grazing + 0.05 * plankton + 0.05 * grazer - 0.1 * q
            x_ref[f * ROWS + r] = total + c(10) * change

    def outer(f):
        at = f // 4 * ROWS
        far, near = halo_ref[f, 0, 0], halo_ref[f, 0, 1]
        x_ref[f * ROWS] += by_member(8, 0, at) * far + by_member(7, 0, at) * near
        x_ref[f * ROWS + 1] += by_member(8, 1, at + 1) * near
        near, far = halo_ref[f, 1, 0], halo_ref[f, 1, 1]
        x_ref[f * ROWS + 2] += by_member(5, 2, at + 2) * near
        x_ref[f * ROWS + 3] += by_member(5, 3, at + 3) * far + by_member(6, 3, at + 3) * near

    f = ORDER[0]
    for side in range(2):
        edges[0, side].wait_recv()
    inner(0, f)
    for side in range(2):
        halos[f, side].wait_recv()
    outer(f)

    fields = jnp.concatenate(
        [
            jnp.concatenate(
                [x_ref[f * ROWS + r], jnp.broadcast_to(ocean[r : r + 1, :], (8, 128))], axis=0
            )
            for r in range(ROWS)
        ],
        axis=1,
    )
    high, mid, low = split3(fields)
    prior = dot_t(own_hot, high) + dot_t(own_hot, mid) + dot_t(own_hot, low)
    rec_ref[...] = jnp.zeros((8, 128), F32)
    rec_ref[:, 0:48] = prior[0:8]
    rec_ref[:, 64:112] = prior[8:16]
    half = gy // 2
    got_ref[1, half, core] = rec_ref[...]
    records = []
    for i, (dc, dj) in enumerate(PARTNERS):
        copy = pltpu.make_async_remote_copy(
            src_ref=rec_ref,
            dst_ref=got_ref.at[1 - dc, half, core],
            send_sem=rec_send.at[i],
            recv_sem=rec_recv.at[i],
            device_id=partner(dc, dj),
            device_id_type=MESH,
        )
        copy.start()
        records.append(copy)

    reach = radius_ref[0] * radius_ref[0]
    upper = jnp.where(big_sub < big_lane, 1.0, 0.0).astype(BF16)

    def before(flag):
        flag = jnp.where(flag, 1.0, 0.0)
        inside = dot(flag.astype(BF16), upper)
        own = jnp.broadcast_to(jnp.sum(flag, axis=1, keepdims=True), (8, 128))
        run = own
        for step in (1, 2, 4):
            run = run + jnp.where(sub >= step, pltpu.roll(run, step, 0), 0.0)
        return inside + run - own, run[7:8, :]

    count_ref[...] = jnp.zeros((8, 128), F32)
    for b in range(2):
        row, col, tile_col, rank = places[b]
        relative = (tile_col - gx + 33) & (TX - 1)
        slot = ((relative * TY + (row >> 2)) * CAP).astype(F32) + rank
        offset = ((col - (col_start + 64) + 2048 + NX) & (NX - 1)) - 2048
        gap_x = jnp.maximum(0, jnp.maximum(offset - 63, -64 - offset))
        gap_y = jnp.maximum(0, jnp.maximum(row - (row_start + 3), row_start - row))
        gap = gap_x * gap_x + gap_y * gap_y
        near = gap < reach
        place, count = before(near)
        place = jnp.where(near, place, -1.0)
        count_ref[2 * b : 2 * b + 1, :] = count
        if b == 0:
            beyond = (gap >= reach) & (gap < 4 * reach)
            place2, count2 = before(beyond)
            place = jnp.where(beyond, place2 + count, place)
            count_ref[1:2, :] = count + count2
        v_ref[0:1, :] = value_ref[b : b + 1, :]
        v_ref[1:2, :] = var_ref[b : b + 1, :]
        rowf, colf = row.astype(F32), col.astype(F32)
        for j in range(CHUNKS):
            window = slice(128 * j, 128 * j + 128)
            v_ref[2:3, window] = rowf[j : j + 1, :]
            v_ref[3:4, window] = colf[j : j + 1, :]
            v_ref[4:5, window] = slot[j : j + 1, :]
        v_ref[5:8, :] = jnp.ones((3, NOBS), F32)
        index = iota((SLOTS, 128), 0).astype(F32)
        for j in range(CHUNKS):
            hot = jnp.where(index == place[j : j + 1, :], 1.0, 0.0)
            hot_ref[:, 128 * j : 128 * j + 128] = hot.astype(BF16)
        hot = hot_ref[...]
        vs = split3(v_ref[...])
        column = dot_t(hot, vs[0]) + dot_t(hot, vs[1]) + dot_t(hot, vs[2])
        row_ref[b] = dot_t(vs[0], hot) + dot_t(vs[1], hot) + dot_t(vs[2], hot)
        ps = split3(pert_ref[b])
        noise = dot(hot, ps[0]) + dot(hot, ps[1]) + dot(hot, ps[2])
        tab_ref[b] = jnp.zeros((SLOTS, 128), F32)
        tab_ref[b, :, 0:M] = column[:, 0:1] + jnp.sqrt(column[:, 1:2]) * noise
        tab_ref[b, :, M : M + 8] = column

    for side in range(2):
        edges[1, side].wait_recv()
    for n, f in enumerate(ORDER):
        if n:
            inner(n, f)
    for copy in records:
        copy.wait_recv()
    swap = pltpu.make_async_remote_copy(
        src_ref=got_ref.at[:, :, core],
        dst_ref=got_ref.at[:, :, core],
        send_sem=swap_send,
        recv_sem=swap_recv,
        device_id=sibling,
        device_id_type=MESH,
    )
    swap.start()
    for f in ORDER[1:]:
        for side in range(2):
            halos[f, side].wait_recv()
        outer(f)
    swap.wait_recv()
    slots_ref[...] = got_ref[...].reshape(SLOTS, 128)
    swap.wait_send()
    for copy in records:
        copy.wait_send()
    for f in ORDER:
        for side in range(2):
            halos[f, side].wait_send()
    for part in range(2):
        for side in range(2):
            edges[part, side].wait_send()


def analysis_kernel(
    x_ref,
    slots_ref,
    tab_ref,
    row_ref,
    count_ref,
    land_ref,
    radius_ref,
    out_ref,
    state_ref,
    part_ref,
    anom_ref,
    scaled_ref,
    innov_ref,
    lhs_ref,
    rhs_ref,
    weight_ref,
    dev_ref,
    out_sem,
):
    gx = lax.axis_index("gx")
    gy = lax.axis_index("gy")
    radius = radius_ref[0].astype(F32)
    per_square = 1.0 / jnp.full((1, 128), radius * radius, F32)
    lane = iota((BLOCK, 128), 1)
    member = lane < M
    counts = [jnp.max(count_ref[i : i + 1, :]).astype(jnp.int32) for i in range(3)]
    blocks0, blocks0_wide, blocks1 = [(n + BLOCK - 1) // BLOCK for n in counts]
    for i, piece in enumerate(split3(slots_ref[...])):
        part_ref[i] = piece
    ocean = land_ref[...].astype(F32)
    exact = functools.partial(
        lax.dot_general, precision=lax.Precision.HIGHEST, preferred_element_type=F32
    )

    def near_x(gap):
        gap = jnp.where(gap >= NX / 2, gap - NX, gap)
        return jnp.where(gap < -NX / 2, gap + NX, gap)

    def load(b, j):
        start = pl.multiple_of(j * BLOCK, BLOCK)
        tab = tab_ref[b, pl.ds(start, BLOCK), :]
        slot = tab[:, M + 4 : M + 5]
        hot = jnp.where(iota((BLOCK, SLOTS), 1).astype(F32) == slot, 1.0, 0.0).astype(BF16)
        prior = dot(hot, part_ref[0]) + dot(hot, part_ref[1]) + dot(hot, part_ref[2])
        if b:
            prior = pltpu.roll(prior, 64, 1)
        return tab, prior

    def finish(b, j, tab, prior):
        prior = jnp.where(member, prior, 0.0)
        anomaly = jnp.where(
            member, prior - jnp.sum(prior, axis=1, keepdims=True) * (1.0 / M), 0.0
        )
        spread = jnp.sum(anomaly * anomaly, axis=1, keepdims=True) * (1.0 / (M - 1))
        filled = tab[:, M + 5 : M + 6]
        scale = filled / ((M - 1) * (spread + tab[:, M + 1 : M + 2] + (1.0 - filled)))
        innovation = jnp.where(member, tab, 0.0) - prior
        if b == 0:
            scaled_ref[j] = anomaly * scale
            innov_ref[j] = innovation
        high = anomaly.astype(BF16).astype(F32)
        lhs = high + pltpu.roll(high, M, 1) + pltpu.roll(anomaly - high, 2 * M, 1)
        anom_ref[b, j] = lhs.astype(BF16)
        turned = innovation.T[0:M, :]
        high = turned.astype(BF16).astype(F32)
        lhs = jnp.concatenate(
            [
                jnp.concatenate([high, high], axis=1),
                jnp.concatenate([turned - high, jnp.zeros_like(high)], axis=1),
            ],
            axis=0,
        )
        lhs_ref[b, j] = lhs.astype(BF16)
        gap = near_x(tab[:, M + 3 : M + 4] - (gx * COLS + lane).astype(F32))
        square = gap * gap
        for r in range(ROWS):
            gap = tab[:, M + 2 : M + 3] - (gy * ROWS + r).astype(F32)
            taper = jnp.maximum(0.0, 1.0 - (square + gap * gap) * per_square)
            weight_ref[b, j, :, 128 * r : 128 * r + 128] = taper * scale

    def first_batch(j, carry):
        tab, prior = load(0, j)
        finish(0, j, tab, prior)
        return carry

    first_batch(0, 0)
    lax.fori_loop(1, blocks0_wide, first_batch, 0)

    def second_batch(j, carry):
        tab, prior = load(1, j)
        wet = prior[:, M : M + 1]
        inside = jnp.where(member, prior, 0.0)
        deviation = jnp.where(
            member, inside - jnp.sum(inside, axis=1, keepdims=True) * (1.0 / M), 0.0
        )

        def add(i, total):
            cover = exact(deviation, scaled_ref[i], (((1,), (1,)), ((), ())))
            window = pl.ds(pl.multiple_of(i * BLOCK, BLOCK), BLOCK)
            gap_x = near_x(row_ref[0, 3:4, window] - tab[:, M + 3 : M + 4])
            gap_y = row_ref[0, 2:3, window] - tab[:, M + 2 : M + 3]
            taper = jnp.maximum(0.0, 1.0 - (gap_x * gap_x + gap_y * gap_y) * per_square)
            return total + exact(cover * taper, innov_ref[i], (((1,), (0,)), ((), ())))

        total = lax.fori_loop(1, blocks0_wide, add, add(0, jnp.zeros((BLOCK, 128), F32)))
        finish(1, j, tab, inside + wet * total)
        return carry

    second_batch(0, 0)
    lax.fori_loop(1, blocks1, second_batch, 0)

    def spread_field(source, f):
        for r in range(ROWS):
            x = source[f * ROWS + r]
            deviation = x - jnp.sum(x, axis=0, keepdims=True) * (1.0 / M)
            high = deviation.astype(BF16).astype(F32)
            stack = jnp.concatenate(
                [high, deviation - high, high, jnp.zeros((8, 128), F32)], axis=0
            )
            dev_ref[f, :, 128 * r : 128 * r + 128] = stack.astype(BF16)

    def increment(b, j, f):
        cover = dot(anom_ref[b, j], dev_ref[f])
        gain = cover * weight_ref[b, j]
        high = gain.astype(BF16)
        low = (gain - high.astype(F32)).astype(BF16)
        both = dot(lhs_ref[b, j], jnp.concatenate([high, low], axis=0))
        return both[0:M] + both[M : 2 * M]

    def apply(b, blocks, source):
        def field(f, carry):
            spread_field(source, f)
            change = increment(b, 0, f)
            for r in range(ROWS):
                state_ref[f * ROWS + r] = (
                    source[f * ROWS + r] + ocean[r : r + 1, :] * change[:, 128 * r : 128 * r + 128]
                )
            return carry

        lax.fori_loop(0, FIELDS, field, 0, unroll=2)

        def more(j, carry):
            def field_more(f, inner_carry):
                change = increment(b, j, f)
                for r in range(ROWS):
                    state_ref[f * ROWS + r] += (
                        ocean[r : r + 1, :] * change[:, 128 * r : 128 * r + 128]
                    )
                return inner_carry

            return lax.fori_loop(0, FIELDS, field_more, carry)

        lax.fori_loop(1, blocks, more, 0)

    apply(0, blocks0, x_ref)
    apply(1, blocks1, state_ref)
    copies = []
    for i in range(FIELDS * ROWS):
        copy = pltpu.make_async_copy(
            state_ref.at[i], out_ref.at[:, i, 0, :], out_sem.at[i]
        )
        copy.start()
        copies.append(copy)
    for copy in copies:
        copy.wait()


def local(
    ensemble,
    courant_x,
    courant_y,
    diffusion,
    mixing,
    growth,
    land_sea,
    obs_cell,
    obs_value,
    observation_variance,
    obs_perturb,
    radius,
):
    vmem = pl.BlockSpec(memory_space=pltpu.VMEM)
    smem = pl.BlockSpec(memory_space=pltpu.SMEM)
    hbm = pl.BlockSpec(memory_space=pl.ANY)
    shape = jax.ShapeDtypeStruct
    dma = pltpu.SemaphoreType.DMA
    x, slots, tab, rows, count = pl.pallas_call(
        forecast_kernel,
        out_shape=(
            shape((FIELDS * ROWS, M, COLS), F32),
            shape((SLOTS, 128), F32),
            shape((2, SLOTS, 128), F32),
            shape((2, 8, SLOTS), F32),
            shape((8, 128), F32),
        ),
        in_specs=[hbm] + [vmem] * 10 + [smem],
        out_specs=(vmem,) * 5,
        scratch_shapes=[
            pltpu.VMEM((FIELDS, ROWS, M, COLS), F32),
            pltpu.VMEM((FIELDS, 2, 2, M, COLS), F32),
            pltpu.VMEM((FIELDS, 8, 128), F32),
            pltpu.VMEM((2, FIELDS, 8, 128), F32),
            pltpu.VMEM((8, 128), F32),
            pltpu.VMEM((3, TY // 2, 2, CAP, 128), F32),
            pltpu.VMEM((2, CHUNKS, 128), jnp.int32),
            pltpu.VMEM((2, CHUNKS, 128), F32),
            pltpu.VMEM((CHUNKS, 128, 128), F32),
            pltpu.VMEM((8, NOBS), F32),
            pltpu.VMEM((SLOTS, NOBS), BF16),
            pltpu.VMEM((2 * ROWS, 12, 8, 128), F32),
            dma((FIELDS, ROWS)),
            dma((FIELDS, 2)),
            dma((FIELDS, 2)),
            dma((2, 2)),
            dma((2, 2)),
            dma((len(PARTNERS),)),
            dma((len(PARTNERS),)),
            dma,
            dma,
        ],
        compiler_params=pltpu.CompilerParams(
            collective_id=0, has_side_effects=True, vmem_limit_bytes=40 << 20
        ),
    )(
        ensemble.reshape(M, FIELDS * ROWS, 1, COLS),
        courant_x.reshape(2 * ROWS, COLS),
        courant_y.reshape(2 * ROWS, COLS),
        diffusion,
        mixing,
        growth.reshape(2 * ROWS, COLS),
        land_sea,
        obs_cell,
        obs_value,
        observation_variance,
        obs_perturb,
        radius,
    )
    most = SLOTS // BLOCK
    out = pl.pallas_call(
        analysis_kernel,
        out_shape=shape((M, FIELDS * ROWS, 1, COLS), F32),
        in_specs=[vmem] * 6 + [smem],
        out_specs=hbm,
        scratch_shapes=[
            pltpu.VMEM((FIELDS * ROWS, M, COLS), F32),
            pltpu.VMEM((3, SLOTS, 128), BF16),
            pltpu.VMEM((2, most, BLOCK, 128), BF16),
            pltpu.VMEM((most, BLOCK, 128), F32),
            pltpu.VMEM((most, BLOCK, 128), F32),
            pltpu.VMEM((2, most, 2 * M, 2 * BLOCK), BF16),
            pltpu.VMEM((8, 128), F32),
            pltpu.VMEM((2, most, BLOCK, ROWS * COLS), F32),
            pltpu.VMEM((FIELDS, 128, ROWS * COLS), BF16),
            dma((FIELDS * ROWS,)),
        ],
        compiler_params=pltpu.CompilerParams(vmem_limit_bytes=40 << 20),
    )(x, slots, tab, rows, count, land_sea, radius)
    return out.reshape(ensemble.shape)


def solution(mesh):
    placed = (
        P(None, None, "gy", "gx"),
        P(None, "gy", "gx"),
        P(None, "gy", "gx"),
        P("gy", "gx"),
        P("gy", "gx"),
        P(None, "gy", "gx"),
        P("gy", "gx"),
        P(),
        P(),
        P(),
        P(),
        P(),
    )
    return jax.shard_map(
        local, mesh=mesh, in_specs=placed, out_specs=P(None, None, "gy", "gx"), check_vma=False
    )
```

time: 206 us -> 49.4 us (0.24)
  blocking collectives: 56.9 us -> 0 us
  starting transfers between devices: 49.2 us -> 0 us
  Pallas kernels: 0 us -> 47.1 us
  matrix products: 44.2 us -> 0 us
  waiting for transfers between devices: 21.6 us -> 0 us
  local copies, waits for them, and re-layouts: 21.7 us -> 1.39 us
  other arithmetic: 10.6 us -> 0 us
    all_gather x2 -> x0, blocking collectives: 56.9 us -> none  [local(): column_slots = lax.all_gather(record, 'gy', axis=1, tiled=True)]
    ppermute x8 -> x0, starting transfers between devices: 49.2 us -> none  [the longest x4 34.2 us: padded_2(): after = lax.ppermute(initial, axis, down)]
    pallas_call x0 -> x2, Pallas kernels: none -> 47.1 us  [the longest x1 39.2 us: local(): pl.pallas_call(forecast_kernel, out_shape=(shape((FIELDS * ROWS, M, COLS)...]
    dot_general x24 -> x0, matrix products: 44.2 us -> none  [the longest x6 21.6 us: local(): lax.dot_general(slot_innov, gain_block, (((0,), (0,)), ((), ())), precisi...]
    ppermute x8 -> x0, waiting for transfers between devices: 21.6 us -> none  [the longest x4 21.6 us: padded_2(): after = lax.ppermute(initial, axis, down)]
    mul x7 -> x0, local copies, waits for them, and re-layouts: 11.4 us -> none  [the longest x6 11.4 us: local(): covariance.reshape(block_size, fields, grid_cell_count) * weight[:, None, :]]
    slice x12 -> x0, local copies, waits for them, and re-layouts: 3.34 us -> none  [the longest x2 1.85 us: padded_2(): last = lax.slice_in_dim(x, length - width, length, axis=dim)]
    mul x4 -> x0, other arithmetic: 3.29 us -> none  [the longest x2 3.05 us: local(): weight = taper_weight * obs_scale[:, None]]
  transfers between devices with their start and end apart: 8 -> 0, of which waited for: 2 -> 0; matrix products, arithmetic and copies ran while one was open for 5% -> 0% of each run, Pallas kernels for 0% -> 0%
where the time goes in v1:
time: 49.4 us; the launch traced here: 49.3 us
  Pallas kernels  47.1 us (95%)
  local copies, waits for them, and re-layouts  1.39 us (3%)
  between operations  0.83 us (2%)
    pallas_call x1, Pallas kernels, local(): pl.pallas_call(forecast_kernel, out_shape=(shape((FIELDS * ROWS, M, COLS)...  39.2 us
    pallas_call x1, Pallas kernels, local(): pl.pallas_call(analysis_kernel, out_shape=shape((M, FIELDS * ROWS, 1, COL...  7.89 us
    unnamed x21, local copies, waits for them, and re-layouts  1.39 us

profile of v1, /device:TPU:1, one launch (start us, length us, event | category | flops | bytes accessed | tf_op | source)
XLA Modules:
  0.0 49.3 jit_solution(10830664457923616555)
XLA Ops:
  0.7 0.0 copy-start
  0.7 0.0 copy-start.1
  0.7 0.0 copy-start.2
  0.7 0.0 copy-start.3
  0.7 0.0 copy-start.4
  0.7 0.0 copy-start.5
  0.7 0.0 copy-start.6
  0.7 0.0 copy-start.7
  0.7 0.0 copy-start.8
  0.7 0.0 copy-start.9
  0.8 1.4 %copy.13.pert_ref = f32[2,1024,40]{2,1,0:T(8,128)S(1)} copy(f32[2,1024,40]{1,2,0:T(8,128)} %param.22) | data formatting | bytes 655360 | tf_op args[10]
  2.1 0.0 copy-done
  2.1 0.0 copy-done.1
  2.1 0.0 copy-done.2
  2.1 0.0 copy-done.3
  2.1 0.0 copy-done.4
  2.2 0.0 copy-done.5
  2.2 0.0 copy-done.6
  2.2 0.0 copy-done.7
  2.2 0.0 copy-done.8
  2.2 0.0 copy-done.9
  2.2 39.2 %shard_map.118 = (f32[32,40,128]{2,1,0:T(8,128)S(1)}, f32[384,128]{1,0:T(8,128)S(1)}, f32[2,384,128]{2,1,0:T(8,128)S(1)}, f32[2,8,384]{2,1,0:T(8,128)S(1)}, f32[8,128]{1,0:T(8,128)S(1)}) custom-call(f32[40,32,1,128]{3,2,1,0:T(1,128)S(1)} %bitcast.5, f32[8,128]{1,0:T(8,128)S(1)} %bitcast.6, f32[8,128]{1,0:T(8,128)S(1)} %bitcast.7, f32[4,128]{1,0:T(4,128)S(1)} %copy-done.8, ...), custom_call_target="tpu_custom_call" | custom-call | tf_op jit(solution)/shard_map/pallas_call | solution.py:611
  41.4 7.9 %shard_map.119 = f32[40,32,1,128]{3,2,1,0:T(1,128)} custom-call(f32[32,40,128]{2,1,0:T(8,128)S(1)} %get-tuple-element.10.x_ref, f32[384,128]{1,0:T(8,128)S(1)} %get-tuple-element.11.slots_ref, f32[2,384,128]{2,1,0:T(8,128)S(1)} %get-tuple-element.12.tab_ref, f32[2,8,384]{2,1,0:T(8,128)S(1)} %get-tuple-element.13.row_ref, ...), custom_call_target="tpu_custom_call" | custom-call | tf_op jit(solution)/shard_map/pallas_call | solution.py:663
Async XLA Ops:
  0.7 1.5 %copy-start = (f32[40,8,4,128]{3,2,1,0:T(4,128)S(1)}, f32[40,8,4,128]{3,2,1,0:T(4,128)}, u32[]{:S(2)}) copy-start(f32[40,8,4,128]{3,2,1,0:T(4,128)} %param.12) | copy-start | bytes 1966084
  0.7 1.5 %copy-start.1 = (s32[2,1024]{1,0:T(2,128)S(1)}, s32[2,1024]{1,0:T(2,128)}, u32[]{:S(2)}) copy-start(s32[2,1024]{1,0:T(2,128)} %cell_ref.1) | copy-start | bytes 24580
  0.7 1.5 %copy-start.2 = (f32[2,1024]{1,0:T(2,128)S(1)}, f32[2,1024]{1,0:T(2,128)}, u32[]{:S(2)}) copy-start(f32[2,1024]{1,0:T(2,128)} %value_ref.1) | copy-start | bytes 24580
  0.7 1.5 %copy-start.3 = (f32[2,1024]{1,0:T(2,128)S(1)}, f32[2,1024]{1,0:T(2,128)}, u32[]{:S(2)}) copy-start(f32[2,1024]{1,0:T(2,128)} %var_ref.1) | copy-start | bytes 24580
  0.7 1.5 %copy-start.4 = (s32[4,128]{1,0:T(4,128)S(1)}, s32[4,128]{1,0:T(4,128)}, u32[]{:S(2)}) copy-start(s32[4,128]{1,0:T(4,128)} %land_ref.3) | copy-start | bytes 6148
  0.7 1.5 %copy-start.5 = (f32[2,4,128]{2,1,0:T(4,128)S(1)}, f32[2,4,128]{2,1,0:T(4,128)}, u32[]{:S(2)}) copy-start(f32[2,4,128]{2,1,0:T(4,128)} %param.13) | copy-start | bytes 12292
  0.7 1.5 %copy-start.6 = (f32[2,4,128]{2,1,0:T(4,128)S(1)}, f32[2,4,128]{2,1,0:T(4,128)}, u32[]{:S(2)}) copy-start(f32[2,4,128]{2,1,0:T(4,128)} %param.14) | copy-start | bytes 12292
  0.7 1.5 %copy-start.7 = (f32[2,4,128]{2,1,0:T(4,128)S(1)}, f32[2,4,128]{2,1,0:T(4,128)}, u32[]{:S(2)}) copy-start(f32[2,4,128]{2,1,0:T(4,128)} %param.17) | copy-start | bytes 12292
  0.7 1.5 %copy-start.8 = (f32[4,128]{1,0:T(4,128)S(1)}, f32[4,128]{1,0:T(4,128)}, u32[]{:S(2)}) copy-start(f32[4,128]{1,0:T(4,128)} %diff_ref.1) | copy-start | bytes 6148
  0.7 1.5 %copy-start.9 = (f32[4,128]{1,0:T(4,128)S(1)}, f32[4,128]{1,0:T(4,128)}, u32[]{:S(2)}) copy-start(f32[4,128]{1,0:T(4,128)} %mix_ref.1) | copy-start | bytes 6148

commit v2 on v1

--- a/solution.py
+++ b/solution.py
@@ -23,6 +23,7 @@
 CHUNKS = NOBS // 128
 BLOCK = 128
 ORDER = (1, 0, 2, 3, 4, 5, 6, 7)
+EARLY = 5
 PARTNERS = [
     (dc, dj) for dj in (4, 3, 5, 2, 6, 1, 7, 0) for dc in (1, -1, 0) if (dc, dj) != (0, 0)
 ]
@@ -50,16 +51,16 @@
 
 def forecast_kernel(
     ens_ref,
-    cx_ref,
-    cy_ref,
-    diff_ref,
-    mix_ref,
-    growth_ref,
-    land_ref,
-    cell_ref,
-    value_ref,
-    var_ref,
-    pert_ref,
+    cx_hbm,
+    cy_hbm,
+    diff_hbm,
+    mix_hbm,
+    growth_hbm,
+    land_hbm,
+    cell_hbm,
+    value_hbm,
+    var_hbm,
+    pert_hbm,
     radius_ref,
     x_ref,
     slots_ref,
@@ -78,6 +79,17 @@
     v_ref,
     hot_ref,
     coef_ref,
+    cx_ref,
+    cy_ref,
+    diff_ref,
+    mix_ref,
+    growth_ref,
+    land_ref,
+    cell_ref,
+    value_ref,
+    var_ref,
+    pert_ref,
+    small_sem,
     load_sem,
     halo_send,
     halo_recv,
@@ -113,11 +125,119 @@
             copy.start()
             loads.append(copy)
 
+    sub = iota((8, 128), 0)
+    lane = iota((8, 128), 1)
+    smalls = []
+    for i, (source, target) in enumerate(
+        (
+            (land_hbm, land_ref),
+            (cx_hbm, cx_ref),
+            (cy_hbm, cy_ref),
+            (diff_hbm, diff_ref),
+            (mix_hbm, mix_ref),
+            (growth_hbm, growth_ref),
+            (cell_hbm, cell_ref),
+            (value_hbm, value_ref),
+            (var_hbm, var_ref),
+            (pert_hbm, pert_ref),
+        )
+    ):
+        copy = pltpu.make_async_copy(source, target, small_sem.at[i])
+        copy.start()
+        smalls.append(copy)
+
+    for n, f in enumerate(ORDER):
+        for r in range(ROWS):
+            loads[n * ROWS + r].wait()
+        packed = jnp.zeros((8, 128), F32)
+        for r in range(ROWS):
+            for i in range(M // 8):
+                at = 4 * (r * (M // 8) + i)
+                moved = pltpu.roll(y_ref[f, r, 8 * i : 8 * i + 8, :], (at + 2) % 128, 1)
+                packed = jnp.where((lane >= at) & (lane < at + 4), moved, packed)
+        edge_ref[n] = packed
+
+    pl.semaphore_wait(barrier, len(PARTNERS) + 2)
+
+    halos = {}
+
+    def send_rows(f):
+        for side, (device, start) in enumerate(((below, 2), (above, 0))):
+            copy = pltpu.make_async_remote_copy(
+                src_ref=y_ref.at[f, pl.ds(start, 2)],
+                dst_ref=halo_ref.at[f, side],
+                send_sem=halo_send.at[f, side],
+                recv_sem=halo_recv.at[f, side],
+                device_id=device,
+                device_id_type=MESH,
+            )
+            copy.start()
+            halos[f, side] = copy
+
+    edges = {}
+
+    def send_edges(part, window):
+        for side, device in enumerate((right, left)):
+            copy = pltpu.make_async_remote_copy(
+                src_ref=edge_ref.at[window],
+                dst_ref=side_ref.at[side, window],
+                send_sem=edge_send.at[part, side],
+                recv_sem=edge_recv.at[part, side],
+                device_id=device,
+                device_id_type=MESH,
+            )
+            copy.start()
+            edges[part, side] = copy
+
+    send_rows(ORDER[0])
+    send_edges(0, pl.ds(0, 1))
+    send_edges(1, pl.ds(1, FIELDS - 1))
+    for f in ORDER[1:EARLY]:
+        send_rows(f)
+
+    for copy in smalls:
+        copy.wait()
+
+    ocean = land_ref[...].astype(F32)
+    first = gy == 0
+    last = gy == TY - 1
+    for level in range(2):
+        for r in range(ROWS):
+            at = level * ROWS + r
+            o = ocean[r : r + 1, :]
+            d = diff_ref[r : r + 1, :] * o
+            cx = cx_ref[at : at + 1, :] * o
+            cy = cy_ref[at : at + 1, :] * o
+            xp, xn = jnp.maximum(cx, 0.0), jnp.minimum(cx, 0.0)
+            yp, yn = jnp.maximum(cy, 0.0), jnp.minimum(cy, 0.0)
+            terms = [
+                1.0 + 0.5 * (xn - xp + yn - yp) - 4.0 * d,
+                xn / 6.0,
+                d - xp / 3.0 - xn,
+                d + xp + xn / 3.0,
+                -xp / 6.0,
+                yn / 6.0,
+                d - yp / 3.0 - yn,
+                d + yp + yn / 3.0,
+                -yp / 6.0,
+            ]
+            if r == 0:
+                terms[7] = jnp.where(first, 0.0, terms[7])
+            if r <= 1:
+                terms[8] = jnp.where(first, 0.0, terms[8])
+            if r == 3:
+                terms[6] = jnp.where(last, 0.0, terms[6])
+            if r >= 2:
+                terms[5] = jnp.where(last, 0.0, terms[5])
+            for i, term in enumerate(terms):
+                coef_ref[at, i] = jnp.broadcast_to(term, (8, 128))
+            coef_ref[at, 9] = jnp.broadcast_to(o * mix_ref[r : r + 1, :], (8, 128))
+            coef_ref[at, 10] = jnp.broadcast_to(o, (8, 128))
+            coef_ref[at, 11] = jnp.broadcast_to(growth_ref[at : at + 1, :], (8, 128))
+
     col_start = gx * COLS
     row_start = gy * ROWS
     me = gx * TY + gy
-    sub = iota((8, 128), 0)
-    lane = iota((8, 128), 1)
     big_sub = iota((128, 128), 0)
     big_lane = iota((128, 128), 1)
     own_hot = []
@@ -155,91 +275,59 @@
         places.append((row, col, tile_col, rank))
     own_hot = jnp.concatenate(own_hot, axis=0).astype(BF16)
 
-    ocean = land_ref[...].astype(F32)
-    first = gy == 0
-    last = gy == TY - 1
-    for level in range(2):
-        for r in range(ROWS):
-            at = level * ROWS + r
-            o = ocean[r : r + 1, :]
-            d = diff_ref[r : r + 1, :] * o
-            cx = cx_ref[at : at + 1, :] * o
-            cy = cy_ref[at : at + 1, :] * o
-            xp, xn = jnp.maximum(cx, 0.0), jnp.minimum(cx, 0.0)
-            yp, yn = jnp.maximum(cy, 0.0), jnp.minimum(cy, 0.0)
-            terms = [
-                1.0 + 0.5 * (xn - xp + yn - yp) - 4.0 * d,
-                xn / 6.0,
-                d - xp / 3.0 - xn,
-                d + xp + xn / 3.0,
-                -xp / 6.0,
-                yn / 6.0,
-                d - yp / 3.0 - yn,
-                d + yp + yn / 3.0,
-                -yp / 6.0,
-            ]
-            if r == 0:
-                terms[7] = jnp.where(first, 0.0, terms[7])
-            if r <= 1:
-                terms[8] = jnp.where(first, 0.0, terms[8])
-            if r == 3:
-                terms[6] = jnp.where(last, 0.0, terms[6])
-            if r >= 2:
-                terms[5] = jnp.where(last, 0.0, terms[5])
-            for i, term in enumerate(terms):
-                coef_ref[at, i] = jnp.broadcast_to(term, (8, 128))
-            coef_ref[at, 9] = jnp.broadcast_to(o * mix_ref[r : r + 1, :], (8, 128))
-            coef_ref[at, 10] = jnp.broadcast_to(o, (8, 128))
-            coef_ref[at, 11] = jnp.broadcast_to(growth_ref[at : at + 1, :], (8, 128))
-
-    for n, f in enumerate(ORDER):
-        for r in range(ROWS):
-            loads[n * ROWS + r].wait()
-        packed = jnp.zeros((8, 128), F32)
-        for r in range(ROWS):
-            for i in range(M // 8):
-                at = 4 * (r * (M // 8) + i)
-                moved = pltpu.roll(y_ref[f, r, 8 * i : 8 * i + 8, :], (at + 2) % 128, 1)
-                packed = jnp.where((lane >= at) & (lane < at + 4), moved, packed)
-        edge_ref[n] = packed
-
-    pl.semaphore_wait(barrier, len(PARTNERS) + 2)
-
-    halos = {}
-
-    def send_rows(f):
-        for side, (device, start) in enumerate(((below, 2), (above, 0))):
-            copy = pltpu.make_async_remote_copy(
-                src_ref=y_ref.at[f, pl.ds(start, 2)],
-                dst_ref=halo_ref.at[f, side],
-                send_sem=halo_send.at[f, side],
-                recv_sem=halo_recv.at[f, side],
-                device_id=device,
-                device_id_type=MESH,
-            )
-            copy.start()
-            halos[f, side] = copy
-
-    edges = {}
-
-    def send_edges(part, window):
-        for side, device in enumerate((right, left)):
-            copy = pltpu.make_async_remote_copy(
-                src_ref=edge_ref.at[window],
-                dst_ref=side_ref.at[side, window],
-                send_sem=edge_send.at[part, side],
-                recv_sem=edge_recv.at[part, side],
-                device_id=device,
-                device_id_type=MESH,
-            )
-            copy.start()
-            edges[part, side] = copy
-
-    send_rows(ORDER[0])
-    send_edges(0, pl.ds(0, 1))
-    send_edges(1, pl.ds(1, FIELDS - 1))
-    for f in ORDER[1:]:
-        send_rows(f)
+    reach = radius_ref[0] * radius_ref[0]
+    upper = jnp.where(big_sub < big_lane, 1.0, 0.0).astype(BF16)
+
+    def before(flag):
+        flag = jnp.where(flag, 1.0, 0.0)
+        inside = dot(flag.astype(BF16), upper)
+        own = jnp.broadcast_to(jnp.sum(flag, axis=1, keepdims=True), (8, 128))
+        run = own
+        for step in (1, 2, 4):
+            run = run + jnp.where(sub >= step, pltpu.roll(run, step, 0), 0.0)
+        return inside + run - own, run[7:8, :]
+
+    count_ref[3:4, :] = jnp.full((1, 128), reach, jnp.int32).astype(F32)
+    count_ref[4:8, :] = ocean
+    for b in range(2):
+        row, col, tile_col, rank = places[b]
+        relative = (tile_col - gx + 33) & (TX - 1)
+        slot = ((relative * TY + (row >> 2)) * CAP).astype(F32) + rank
+        offset = ((col - (col_start + 64) + 2048 + NX) & (NX - 1)) - 2048
+        gap_x = jnp.maximum(0, jnp.maximum(offset - 63, -64 - offset))
+        gap_y = jnp.maximum(0, jnp.maximum(row - (row_start + 3), row_start - row))
+        gap = gap_x * gap_x + gap_y * gap_y
+        near = gap < reach
+        place, count = before(near)
+        place = jnp.where(near, place, -1.0)
+        count_ref[2 * b : 2 * b + 1, :] = count
+        if b == 0:
+            beyond = (gap >= reach) & (gap < 4 * reach)
+            place2, count2 = before(beyond)
+            place = jnp.where(beyond, place2 + count, place)
+            count_ref[1:2, :] = count + count2
+        v_ref[0:1, :] = value_ref[b : b + 1, :]
+        v_ref[1:2, :] = var_ref[b : b + 1, :]
+        rowf, colf = row.astype(F32), col.astype(F32)
+        for j in range(CHUNKS):
+            window = slice(128 * j, 128 * j + 128)
+            v_ref[2:3, window] = rowf[j : j + 1, :]
+            v_ref[3:4, window] = colf[j : j + 1, :]
+            v_ref[4:5, window] = slot[j : j + 1, :]
+        v_ref[5:8, :] = jnp.ones((3, NOBS), F32)
+        index = iota((SLOTS, 128), 0).astype(F32)
+        for j in range(CHUNKS):
+            hot = jnp.where(index == place[j : j + 1, :], 1.0, 0.0)
+            hot_ref[:, 128 * j : 128 * j + 128] = hot.astype(BF16)
+        hot = hot_ref[...]
+        vs = split3(v_ref[...])
+        column = dot_t(hot, vs[0]) + dot_t(hot, vs[1]) + dot_t(hot, vs[2])
+        row_ref[b] = dot_t(vs[0], hot) + dot_t(vs[1], hot) + dot_t(vs[2], hot)
+        ps = split3(pert_ref[b])
+        noise = dot_t(hot, ps[0]) + dot_t(hot, ps[1]) + dot_t(hot, ps[2])
+        tab_ref[b] = jnp.zeros((SLOTS, 128), F32)
+        tab_ref[b, :, 0:M] = column[:, 0:1] + jnp.sqrt(column[:, 1:2]) * noise
+        tab_ref[b, :, M : M + 8] = column
 
     def by_member(value, r, at):
         return jnp.broadcast_to(coef_ref[at, value][None], (M // 8, 8, 128)).reshape(M, 128)
@@ -334,65 +422,18 @@
         )
         copy.start()
         records.append(copy)
-
-    reach = radius_ref[0] * radius_ref[0]
-    upper = jnp.where(big_sub < big_lane, 1.0, 0.0).astype(BF16)
-
-    def before(flag):
-        flag = jnp.where(flag, 1.0, 0.0)
-        inside = dot(flag.astype(BF16), upper)
-        own = jnp.broadcast_to(jnp.sum(flag, axis=1, keepdims=True), (8, 128))
-        run = own
-        for step in (1, 2, 4):
-            run = run + jnp.where(sub >= step, pltpu.roll(run, step, 0), 0.0)
-        return inside + run - own, run[7:8, :]
-
-    count_ref[...] = jnp.zeros((8, 128), F32)
-    for b in range(2):
-        row, col, tile_col, rank = places[b]
-        relative = (tile_col - gx + 33) & (TX - 1)
-        slot = ((relative * TY + (row >> 2)) * CAP).astype(F32) + rank
-        offset = ((col - (col_start + 64) + 2048 + NX) & (NX - 1)) - 2048
-        gap_x = jnp.maximum(0, jnp.maximum(offset - 63, -64 - offset))
-        gap_y = jnp.maximum(0, jnp.maximum(row - (row_start + 3), row_start - row))
-        gap = gap_x * gap_x + gap_y * gap_y
-        near = gap < reach
-        place, count = before(near)
-        place = jnp.where(near, place, -1.0)
-        count_ref[2 * b : 2 * b + 1, :] = count
-        if b == 0:
-            beyond = (gap >= reach) & (gap < 4 * reach)
-            place2, count2 = before(beyond)
-            place = jnp.where(beyond, place2 + count, place)
-            count_ref[1:2, :] = count + count2
-        v_ref[0:1, :] = value_ref[b : b + 1, :]
-        v_ref[1:2, :] = var_ref[b : b + 1, :]
-        rowf, colf = row.astype(F32), col.astype(F32)
-        for j in range(CHUNKS):
-            window = slice(128 * j, 128 * j + 128)
-            v_ref[2:3, window] = rowf[j : j + 1, :]
-            v_ref[3:4, window] = colf[j : j + 1, :]
-            v_ref[4:5, window] = slot[j : j + 1, :]
-        v_ref[5:8, :] = jnp.ones((3, NOBS), F32)
-        index = iota((SLOTS, 128), 0).astype(F32)
-        for j in range(CHUNKS):
-            hot = jnp.where(index == place[j : j + 1, :], 1.0, 0.0)
-            hot_ref[:, 128 * j : 128 * j + 128] = hot.astype(BF16)
-        hot = hot_ref[...]
-        vs = split3(v_ref[...])
-        column = dot_t(hot, vs[0]) + dot_t(hot, vs[1]) + dot_t(hot, vs[2])
-        row_ref[b] = dot_t(vs[0], hot) + dot_t(vs[1], hot) + dot_t(vs[2], hot)
-        ps = split3(pert_ref[b])
-        noise = dot(hot, ps[0]) + dot(hot, ps[1]) + dot(hot, ps[2])
-        tab_ref[b] = jnp.zeros((SLOTS, 128), F32)
-        tab_ref[b, :, 0:M] = column[:, 0:1] + jnp.sqrt(column[:, 1:2]) * noise
-        tab_ref[b, :, M : M + 8] = column
+    for f in ORDER[EARLY:]:
+        send_rows(f)
 
     for side in range(2):
         edges[1, side].wait_recv()
     for n, f in enumerate(ORDER):
         if n:
             inner(n, f)
+    for f in ORDER[1:EARLY]:
+        for side in range(2):
+            halos[f, side].wait_recv()
+        outer(f)
     for copy in records:
         copy.wait_recv()
     swap = pltpu.make_async_remote_copy(
@@ -404,7 +445,7 @@
         device_id_type=MESH,
     )
     swap.start()
-    for f in ORDER[1:]:
+    for f in ORDER[EARLY:]:
         for side in range(2):
             halos[f, side].wait_recv()
         outer(f)
@@ -427,8 +468,6 @@
     tab_ref,
     row_ref,
     count_ref,
-    land_ref,
-    radius_ref,
     out_ref,
     state_ref,
     part_ref,
@@ -436,22 +475,20 @@
     scaled_ref,
     innov_ref,
     lhs_ref,
-    rhs_ref,
     weight_ref,
     dev_ref,
     out_sem,
 ):
     gx = lax.axis_index("gx")
     gy = lax.axis_index("gy")
-    radius = radius_ref[0].astype(F32)
-    per_square = 1.0 / jnp.full((1, 128), radius * radius, F32)
+    per_square = 1.0 / count_ref[3:4, :]
     lane = iota((BLOCK, 128), 1)
     member = lane < M
     counts = [jnp.max(count_ref[i : i + 1, :]).astype(jnp.int32) for i in range(3)]
     blocks0, blocks0_wide, blocks1 = [(n + BLOCK - 1) // BLOCK for n in counts]
     for i, piece in enumerate(split3(slots_ref[...])):
         part_ref[i] = piece
-    ocean = land_ref[...].astype(F32)
+    ocean = count_ref[4:8, :]
     exact = functools.partial(
         lax.dot_general, precision=lax.Precision.HIGHEST, preferred_element_type=F32
     )
@@ -510,30 +547,32 @@
     first_batch(0, 0)
     lax.fori_loop(1, blocks0_wide, first_batch, 0)
 
+    def deviation_of(prior):
+        inside = jnp.where(member, prior, 0.0)
+        mean = jnp.sum(inside, axis=1, keepdims=True) * (1.0 / M)
+        return inside, jnp.where(member, inside - mean, 0.0)
+
+    def effect(i, tab, deviation):
+        cover = exact(deviation, scaled_ref[i], (((1,), (1,)), ((), ())))
+        window = pl.ds(pl.multiple_of(i * BLOCK, BLOCK), BLOCK)
+        gap_x = near_x(row_ref[0, 3:4, window] - tab[:, M + 3 : M + 4])
+        gap_y = row_ref[0, 2:3, window] - tab[:, M + 2 : M + 3]
+        taper = jnp.maximum(0.0, 1.0 - (gap_x * gap_x + gap_y * gap_y) * per_square)
+        return exact(cover * taper, innov_ref[i], (((1,), (0,)), ((), ())))
+
     def second_batch(j, carry):
         tab, prior = load(1, j)
-        wet = prior[:, M : M + 1]
-        inside = jnp.where(member, prior, 0.0)
-        deviation = jnp.where(
-            member, inside - jnp.sum(inside, axis=1, keepdims=True) * (1.0 / M), 0.0
+        inside, deviation = deviation_of(prior)
+        total = lax.fori_loop(
+            1,
+            blocks0_wide,
+            lambda i, total: total + effect(i, tab, deviation),
+            effect(0, tab, deviation),
         )
-
-        def add(i, total):
-            cover = exact(deviation, scaled_ref[i], (((1,), (1,)), ((), ())))
-            window = pl.ds(pl.multiple_of(i * BLOCK, BLOCK), BLOCK)
-            gap_x = near_x(row_ref[0, 3:4, window] - tab[:, M + 3 : M + 4])
-            gap_y = row_ref[0, 2:3, window] - tab[:, M + 2 : M + 3]
-            taper = jnp.maximum(0.0, 1.0 - (gap_x * gap_x + gap_y * gap_y) * per_square)
-            return total + exact(cover * taper, innov_ref[i], (((1,), (0,)), ((), ())))
-
-        total = lax.fori_loop(1, blocks0_wide, add, add(0, jnp.zeros((BLOCK, 128), F32)))
-        finish(1, j, tab, inside + wet * total)
+        finish(1, j, tab, inside + prior[:, M : M + 1] * total)
         return carry
 
-    second_batch(0, 0)
-    lax.fori_loop(1, blocks1, second_batch, 0)
-
-    def spread_field(source, f):
+    def spread_field(b, source, f):
         for r in range(ROWS):
             x = source[f * ROWS + r]
             deviation = x - jnp.sum(x, axis=0, keepdims=True) * (1.0 / M)
@@ -541,52 +580,78 @@
             stack = jnp.concatenate(
                 [high, deviation - high, high, jnp.zeros((8, 128), F32)], axis=0
             )
-            dev_ref[f, :, 128 * r : 128 * r + 128] = stack.astype(BF16)
+            dev_ref[b, f, :, 128 * r : 128 * r + 128] = stack.astype(BF16)
 
     def increment(b, j, f):
-        cover = dot(anom_ref[b, j], dev_ref[f])
+        cover = dot(anom_ref[b, j], dev_ref[b, f])
         gain = cover * weight_ref[b, j]
         high = gain.astype(BF16)
         low = (gain - high.astype(F32)).astype(BF16)
         both = dot(lhs_ref[b, j], jnp.concatenate([high, low], axis=0))
         return both[0:M] + both[M : 2 * M]
 
-    def apply(b, blocks, source):
-        def field(f, carry):
-            spread_field(source, f)
-            change = increment(b, 0, f)
-            for r in range(ROWS):
-                state_ref[f * ROWS + r] = (
-                    source[f * ROWS + r] + ocean[r : r + 1, :] * change[:, 128 * r : 128 * r + 128]
-                )
-            return carry
-
-        lax.fori_loop(0, FIELDS, field, 0, unroll=2)
-
-        def more(j, carry):
-            def field_more(f, inner_carry):
-                change = increment(b, j, f)
-                for r in range(ROWS):
-                    state_ref[f * ROWS + r] += (
-                        ocean[r : r + 1, :] * change[:, 128 * r : 128 * r + 128]
-                    )
-                return inner_carry
-
-            return lax.fori_loop(0, FIELDS, field_more, carry)
-
-        lax.fori_loop(1, blocks, more, 0)
-
-    apply(0, blocks0, x_ref)
-    apply(1, blocks1, state_ref)
-    copies = []
+    def apply_field(b, source, f):
+        spread_field(b, source, f)
+        change = increment(b, 0, f)
+        for r in range(ROWS):
+            state_ref[f * ROWS + r] = (
+                source[f * ROWS + r] + ocean[r : r + 1, :] * change[:, 128 * r : 128 * r + 128]
+            )
+
+    def store(f):
+        for r in range(ROWS):
+            i = f * ROWS + r
+            pltpu.make_async_copy(state_ref.at[i], out_ref.at[:, i, 0, :], out_sem.at[i]).start()
+
+    short = (blocks0 <= 1) & (blocks1 <= 1)
+
+    @pl.when(short)
+    def _():
+        tab, prior = load(1, 0)
+        inside, deviation = deviation_of(prior)
+        extra = lax.fori_loop(
+            1,
+            blocks0_wide,
+            lambda i, total: total + effect(i, tab, deviation),
+            jnp.zeros((BLOCK, 128), F32),
+        )
+        total = extra + effect(0, tab, deviation)
+        finish(1, 0, tab, inside + prior[:, M : M + 1] * total)
+        for f in range(FIELDS):
+            apply_field(0, x_ref, f)
+        for f in range(FIELDS):
+            apply_field(1, state_ref, f)
+            store(f)
+
+    @pl.when(jnp.logical_not(short))
+    def _():
+        second_batch(0, 0)
+        lax.fori_loop(1, blocks1, second_batch, 0)
+        for b, blocks, source in ((0, blocks0, x_ref), (1, blocks1, state_ref)):
+
+            def field(f, carry, b=b, source=source):
+                apply_field(b, source, f)
+                return carry
+
+            lax.fori_loop(0, FIELDS, field, 0)
+
+            def more(j, carry, b=b):
+                def field_more(f, inner_carry):
+                    change = increment(b, j, f)
+                    for r in range(ROWS):
+                        state_ref[f * ROWS + r] += (
+                            ocean[r : r + 1, :] * change[:, 128 * r : 128 * r + 128]
+                        )
+                    return inner_carry
+
+                return lax.fori_loop(0, FIELDS, field_more, carry)
+
+            lax.fori_loop(1, blocks, more, 0)
+        for f in range(FIELDS):
+            store(f)
+
     for i in range(FIELDS * ROWS):
-        copy = pltpu.make_async_copy(
-            state_ref.at[i], out_ref.at[:, i, 0, :], out_sem.at[i]
-        )
-        copy.start()
-        copies.append(copy)
-    for copy in copies:
-        copy.wait()
+        pltpu.make_async_copy(state_ref.at[i], out_ref.at[:, i, 0, :], out_sem.at[i]).wait()
 
 
 def local(
@@ -604,8 +669,7 @@
     radius,
 ):
     vmem = pl.BlockSpec(memory_space=pltpu.VMEM)
-    smem = pl.BlockSpec(memory_space=pltpu.SMEM)
-    hbm = pl.BlockSpec(memory_space=pl.ANY)
+    hbm = pl.BlockSpec(memory_space=pltpu.HBM)
     shape = jax.ShapeDtypeStruct
     dma = pltpu.SemaphoreType.DMA
     x, slots, tab, rows, count = pl.pallas_call(
@@ -617,7 +681,7 @@
             shape((2, 8, SLOTS), F32),
             shape((8, 128), F32),
         ),
-        in_specs=[hbm] + [vmem] * 10 + [smem],
+        in_specs=[hbm] * 11 + [pl.BlockSpec(memory_space=pltpu.SMEM)],
         out_specs=(vmem,) * 5,
         scratch_shapes=[
             pltpu.VMEM((FIELDS, ROWS, M, COLS), F32),
@@ -632,6 +696,17 @@
             pltpu.VMEM((8, NOBS), F32),
             pltpu.VMEM((SLOTS, NOBS), BF16),
             pltpu.VMEM((2 * ROWS, 12, 8, 128), F32),
+            pltpu.VMEM((2 * ROWS, COLS), F32),
+            pltpu.VMEM((2 * ROWS, COLS), F32),
+            pltpu.VMEM((ROWS, COLS), F32),
+            pltpu.VMEM((ROWS, COLS), F32),
+            pltpu.VMEM((2 * ROWS, COLS), F32),
+            pltpu.VMEM((ROWS, COLS), jnp.int32),
+            pltpu.VMEM((2, NOBS), jnp.int32),
+            pltpu.VMEM((2, NOBS), F32),
+            pltpu.VMEM((2, NOBS), F32),
+            pltpu.VMEM((2, M, NOBS), F32),
+            dma((10,)),
             dma((FIELDS, ROWS)),
             dma((FIELDS, 2)),
             dma((FIELDS, 2)),
@@ -646,24 +721,29 @@
             collective_id=0, has_side_effects=True, vmem_limit_bytes=40 << 20
         ),
     )(
-        ensemble.reshape(M, FIELDS * ROWS, 1, COLS),
-        courant_x.reshape(2 * ROWS, COLS),
-        courant_y.reshape(2 * ROWS, COLS),
-        diffusion,
-        mixing,
-        growth.reshape(2 * ROWS, COLS),
-        land_sea,
-        obs_cell,
-        obs_value,
-        observation_variance,
-        obs_perturb,
+        *(
+            pltpu.with_memory_space_constraint(array, pltpu.HBM)
+            for array in (
+                ensemble.reshape(M, FIELDS * ROWS, 1, COLS),
+                courant_x.reshape(2 * ROWS, COLS),
+                courant_y.reshape(2 * ROWS, COLS),
+                diffusion,
+                mixing,
+                growth.reshape(2 * ROWS, COLS),
+                land_sea,
+                obs_cell,
+                obs_value,
+                observation_variance,
+                jnp.swapaxes(obs_perturb, 1, 2),
+            )
+        ),
         radius,
     )
     most = SLOTS // BLOCK
     out = pl.pallas_call(
         analysis_kernel,
         out_shape=shape((M, FIELDS * ROWS, 1, COLS), F32),
-        in_specs=[vmem] * 6 + [smem],
+        in_specs=[vmem] * 5,
         out_specs=hbm,
         scratch_shapes=[
             pltpu.VMEM((FIELDS * ROWS, M, COLS), F32),
@@ -672,13 +752,12 @@
             pltpu.VMEM((most, BLOCK, 128), F32),
             pltpu.VMEM((most, BLOCK, 128), F32),
             pltpu.VMEM((2, most, 2 * M, 2 * BLOCK), BF16),
-            pltpu.VMEM((8, 128), F32),
             pltpu.VMEM((2, most, BLOCK, ROWS * COLS), F32),
-            pltpu.VMEM((FIELDS, 128, ROWS * COLS), BF16),
+            pltpu.VMEM((2, FIELDS, 128, ROWS * COLS), BF16),
             dma((FIELDS * ROWS,)),
         ],
         compiler_params=pltpu.CompilerParams(vmem_limit_bytes=40 << 20),
-    )(x, slots, tab, rows, count, land_sea, radius)
+    )(x, slots, tab, rows, count)
     return out.reshape(ensemble.shape)
 
 

time: 49.4 us -> 42.8 us (0.87)
  Pallas kernels: 47.1 us -> 42 us
  local copies, waits for them, and re-layouts: 1.39 us -> 0 us
    pallas_call x1, Pallas kernels: 39.2 us -> 36.3 us  [local(): pl.pallas_call(forecast_kernel, out_shape=(shape((FIELDS * ROWS, M, COLS)...]
    pallas_call x1, Pallas kernels: 7.89 us -> 5.7 us  [local(): pl.pallas_call(analysis_kernel, out_shape=shape((M, FIELDS * ROWS, 1, COL...]
    unnamed x21 -> x0, local copies, waits for them, and re-layouts: 1.39 us -> none
where the time goes in v2:
time: 42.8 us; the launch traced here: 42.7 us
  Pallas kernels  42 us (98%)
  between operations  0.66 us (2%)
    pallas_call x1, Pallas kernels, local(): pl.pallas_call(forecast_kernel, out_shape=(shape((FIELDS * ROWS, M, COLS)...  36.3 us
    pallas_call x1, Pallas kernels, local(): pl.pallas_call(analysis_kernel, out_shape=shape((M, FIELDS * ROWS, 1, COL...  5.7 us

profile of v2, /device:TPU:1, one launch (start us, length us, event | category | flops | bytes accessed | tf_op | source)
XLA Modules:
  0.0 42.7 jit_solution(8750203367009218416)
XLA Ops:
  0.7 36.3 %shard_map.118 = (f32[32,40,128]{2,1,0:T(8,128)S(1)}, f32[384,128]{1,0:T(8,128)S(1)}, f32[2,384,128]{2,1,0:T(8,128)S(1)}, f32[2,8,384]{2,1,0:T(8,128)S(1)}, f32[8,128]{1,0:T(8,128)S(1)}) custom-call(f32[40,32,1,128]{3,2,1,0:T(1,128)} %bitcast.6, f32[8,128]{1,0:T(8,128)} %bitcast.8, f32[8,128]{1,0:T(8,128)} %bitcast.9, f32[4,128]{1,0:T(4,128)} %diff_hbm.1, ...), custom_call_target="tpu_custom_call" | custom-call | tf_op jit(solution)/shard_map/pallas_call | solution.py:675
  37.0 5.7 %shard_map.119 = f32[40,32,1,128]{3,2,1,0:T(1,128)} custom-call(f32[32,40,128]{2,1,0:T(8,128)S(1)} %get-tuple-element.10.x_ref, f32[384,128]{1,0:T(8,128)S(1)} %get-tuple-element.11.slots_ref, f32[2,384,128]{2,1,0:T(8,128)S(1)} %get-tuple-element.12.tab_ref, f32[2,8,384]{2,1,0:T(8,128)S(1)} %get-tuple-element.13.row_ref, ...), custom_call_target="tpu_custom_call" | custom-call | tf_op jit(solution)/shard_map/pallas_call | solution.py:743

commit v3 on v2

--- a/solution.py
+++ b/solution.py
@@ -22,8 +22,9 @@
 SLOTS = 3 * TY * CAP
 CHUNKS = NOBS // 128
 BLOCK = 128
+WIDE = 2
 ORDER = (1, 0, 2, 3, 4, 5, 6, 7)
-EARLY = 5
+EARLY = 4
 PARTNERS = [
     (dc, dj) for dj in (4, 3, 5, 2, 6, 1, 7, 0) for dc in (1, -1, 0) if (dc, dj) != (0, 0)
 ]
@@ -47,6 +48,190 @@
 
 def iota(shape, dim):
     return lax.broadcasted_iota(jnp.int32, shape, dim)
+
+
+class Analysis:
+    def __init__(self, tab, row, count, part, anom, scaled, innov, lhs, weight, dev, state):
+        self.tab, self.row, self.part = tab, row, part
+        self.anom, self.scaled, self.innov = anom, scaled, innov
+        self.lhs, self.weight, self.dev, self.state = lhs, weight, dev, state
+        self.gx, self.gy = lax.axis_index("gx"), lax.axis_index("gy")
+        self.lane = iota((BLOCK, 128), 1)
+        self.member = self.lane < M
+        self.per_square = 1.0 / count[3:4, :]
+        self.ocean = count[4:8, :]
+        self.exact = functools.partial(
+            lax.dot_general, precision=lax.Precision.HIGHEST, preferred_element_type=F32
+        )
+
+    def near_x(self, gap):
+        gap = jnp.where(gap >= NX / 2, gap - NX, gap)
+        return jnp.where(gap < -NX / 2, gap + NX, gap)
+
+    def load(self, b, j):
+        start = j * BLOCK if isinstance(j, int) else pl.multiple_of(j * BLOCK, BLOCK)
+        tab = self.tab[b, pl.ds(start, BLOCK), :]
+        slot = tab[:, M + 4 : M + 5]
+        hot = jnp.where(iota((BLOCK, SLOTS), 1).astype(F32) == slot, 1.0, 0.0).astype(BF16)
+        prior = dot(hot, self.part[0]) + dot(hot, self.part[1]) + dot(hot, self.part[2])
+        if b:
+            prior = pltpu.roll(prior, 64, 1)
+        return tab, prior
+
+    def deviation_of(self, prior):
+        inside = jnp.where(self.member, prior, 0.0)
+        mean = jnp.sum(inside, axis=1, keepdims=True) * (1.0 / M)
+        return inside, jnp.where(self.member, inside - mean, 0.0)
+
+    def finish(self, b, j, tab, prior, grid=True):
+        prior, anomaly = self.deviation_of(prior)
+        spread = jnp.sum(anomaly * anomaly, axis=1, keepdims=True) * (1.0 / (M - 1))
+        filled = tab[:, M + 5 : M + 6]
+        scale = filled / ((M - 1) * (spread + tab[:, M + 1 : M + 2] + (1.0 - filled)))
+        innovation = jnp.where(self.member, tab, 0.0) - prior
+        if b == 0:
+            self.scaled[j] = anomaly * scale
+            self.innov[j] = innovation
+        if not grid:
+            return
+        high = anomaly.astype(BF16).astype(F32)
+        lhs = high + pltpu.roll(high, M, 1) + pltpu.roll(anomaly - high, 2 * M, 1)
+        self.anom[b, j] = lhs.astype(BF16)
+        turned = innovation.T[0:M, :]
+        high = turned.astype(BF16).astype(F32)
+        lhs = jnp.concatenate(
+            [
+                jnp.concatenate([high, high], axis=1),
+                jnp.concatenate([turned - high, jnp.zeros_like(high)], axis=1),
+            ],
+            axis=0,
+        )
+        self.lhs[b, j] = lhs.astype(BF16)
+        gap = self.near_x(tab[:, M + 3 : M + 4] - (self.gx * COLS + self.lane).astype(F32))
+        square = gap * gap
+        for r in range(ROWS):
+            gap = tab[:, M + 2 : M + 3] - (self.gy * ROWS + r).astype(F32)
+            taper = jnp.maximum(0.0, 1.0 - (square + gap * gap) * self.per_square)
+            self.weight[b, j, :, 128 * r : 128 * r + 128] = taper * scale
+
+    def effect(self, i, tab, deviation):
+        cover = self.exact(deviation, self.scaled[i], (((1,), (1,)), ((), ())))
+        start = i * BLOCK if isinstance(i, int) else pl.multiple_of(i * BLOCK, BLOCK)
+        window = pl.ds(start, BLOCK)
+        gap_x = self.near_x(self.row[0, 3:4, window] - tab[:, M + 3 : M + 4])
+        gap_y = self.row[0, 2:3, window] - tab[:, M + 2 : M + 3]
+        taper = jnp.maximum(0.0, 1.0 - (gap_x * gap_x + gap_y * gap_y) * self.per_square)
+        return self.exact(cover * taper, self.innov[i], (((1,), (0,)), ((), ())))
+
+    def spread_field(self, b, source, f):
+        for r in range(ROWS):
+            x = source[f * ROWS + r]
+            deviation = x - jnp.sum(x, axis=0, keepdims=True) * (1.0 / M)
+            high = deviation.astype(BF16).astype(F32)
+            stack = jnp.concatenate(
+                [high, deviation - high, high, jnp.zeros((8, 128), F32)], axis=0
+            )
+            self.dev[b, f, :, 128 * r : 128 * r + 128] = stack.astype(BF16)
+
+    def increment(self, b, j, f):
+        cover = dot(self.anom[b, j], self.dev[b, f])
+        gain = cover * self.weight[b, j]
+        high = gain.astype(BF16)
+        low = (gain - high.astype(F32)).astype(BF16)
+        both = dot(self.lhs[b, j], jnp.concatenate([high, low], axis=0))
+        return both[0:M] + both[M : 2 * M]
+
+    def apply_field(self, b, source, f):
+        change = self.increment(b, 0, f)
+        for r in range(ROWS):
+            self.state[f * ROWS + r] = (
+                source[f * ROWS + r]
+                + self.ocean[r : r + 1, :] * change[:, 128 * r : 128 * r + 128]
+            )
+
+
+def analysis_kernel(
+    done_ref,
+    x_ref,
+    slots_ref,
+    tab_ref,
+    row_ref,
+    count_ref,
+    out_ref,
+    part_ref,
+    anom_ref,
+    scaled_ref,
+    innov_ref,
+    lhs_ref,
+    weight_ref,
+    dev_ref,
+    state_ref,
+    out_sem,
+):
+    def stores(source):
+        for i in range(FIELDS * ROWS):
+            yield pltpu.make_async_copy(source.at[i], out_ref.at[:, i, 0, :], out_sem.at[i])
+
+    for copy in stores(done_ref):
+        copy.start()
+    counts = [jnp.max(count_ref[i : i + 1, :]).astype(jnp.int32) for i in range(3)]
+    blocks0, blocks0_wide, blocks1 = [(n + BLOCK - 1) // BLOCK for n in counts]
+    for copy in stores(done_ref):
+        copy.wait()
+
+    @pl.when((blocks0 > 1) | (blocks0_wide > WIDE) | (blocks1 > 1))
+    def _():
+        a = Analysis(
+            tab_ref, row_ref, count_ref, part_ref, anom_ref, scaled_ref, innov_ref, lhs_ref,
+            weight_ref, dev_ref, state_ref,
+        )
+        for i, piece in enumerate(split3(slots_ref[...])):
+            part_ref[i] = piece
+
+        def first_batch(j, carry):
+            a.finish(0, j, *a.load(0, j))
+            return carry
+
+        lax.fori_loop(0, blocks0_wide, first_batch, 0)
+
+        def second_batch(j, carry):
+            tab, prior = a.load(1, j)
+            inside, deviation = a.deviation_of(prior)
+            total = lax.fori_loop(
+                0,
+                blocks0_wide,
+                lambda i, total: total + a.effect(i, tab, deviation),
+                jnp.zeros((BLOCK, 128), F32),
+            )
+            a.finish(1, j, tab, inside + prior[:, M : M + 1] * total)
+            return carry
+
+        lax.fori_loop(0, blocks1, second_batch, 0)
+        state_ref[...] = x_ref[...]
+        for b, blocks in ((0, blocks0), (1, blocks1)):
+
+            def spread(f, carry, b=b):
+                a.spread_field(b, state_ref, f)
+                return carry
+
+            lax.fori_loop(0, FIELDS, spread, 0)
+
+            def block(j, carry, b=b):
+                def field(f, inner_carry):
+                    change = a.increment(b, j, f)
+                    for r in range(ROWS):
+                        state_ref[f * ROWS + r] += (
+                            a.ocean[r : r + 1, :] * change[:, 128 * r : 128 * r + 128]
+                        )
+                    return inner_carry
+
+                return lax.fori_loop(0, FIELDS, field, carry)
+
+            lax.fori_loop(0, blocks, block, 0)
+        for copy in stores(state_ref):
+            copy.start()
+        for copy in stores(state_ref):
+            copy.wait()
 
 
 def forecast_kernel(
@@ -62,6 +247,7 @@
     var_hbm,
     pert_hbm,
     radius_ref,
+    done_ref,
     x_ref,
     slots_ref,
     tab_ref,
@@ -89,6 +275,13 @@
     value_ref,
     var_ref,
     pert_ref,
+    part_ref,
+    anom_ref,
+    scaled_ref,
+    innov_ref,
+    lhs_ref,
+    weight_ref,
+    dev_ref,
     small_sem,
     load_sem,
     halo_send,
@@ -422,8 +615,6 @@
         )
         copy.start()
         records.append(copy)
-    for f in ORDER[EARLY:]:
-        send_rows(f)
 
     for side in range(2):
         edges[1, side].wait_recv()
@@ -434,6 +625,14 @@
         for side in range(2):
             halos[f, side].wait_recv()
         outer(f)
+    a = Analysis(
+        tab_ref, row_ref, count_ref, part_ref, anom_ref, scaled_ref, innov_ref, lhs_ref,
+        weight_ref, dev_ref, done_ref,
+    )
+    for f in ORDER[:EARLY]:
+        a.spread_field(0, x_ref, f)
+    for f in ORDER[EARLY:]:
+        send_rows(f)
     for copy in records:
         copy.wait_recv()
     swap = pltpu.make_async_remote_copy(
@@ -445,12 +644,32 @@
         device_id_type=MESH,
     )
     swap.start()
+    swap.wait_recv()
+
+    slots_ref[...] = got_ref[...].reshape(SLOTS, 128)
+    for i, piece in enumerate(split3(slots_ref[...])):
+        part_ref[i] = piece
+    for j in range(WIDE):
+        a.finish(0, j, *a.load(0, j), grid=j == 0)
+    tab, prior = a.load(1, 0)
+    inside, deviation = a.deviation_of(prior)
+    total = sum(a.effect(j, tab, deviation) for j in range(WIDE))
+    a.finish(1, 0, tab, inside + prior[:, M : M + 1] * total)
+    for f in ORDER[:EARLY]:
+        a.apply_field(0, x_ref, f)
+    for f in ORDER[:EARLY]:
+        a.spread_field(1, done_ref, f)
+        a.apply_field(1, done_ref, f)
     for f in ORDER[EARLY:]:
         for side in range(2):
             halos[f, side].wait_recv()
         outer(f)
-    swap.wait_recv()
-    slots_ref[...] = got_ref[...].reshape(SLOTS, 128)
+        a.spread_field(0, x_ref, f)
+    for f in ORDER[EARLY:]:
+        a.apply_field(0, x_ref, f)
+    for f in ORDER[EARLY:]:
+        a.spread_field(1, done_ref, f)
+        a.apply_field(1, done_ref, f)
     swap.wait_send()
     for copy in records:
         copy.wait_send()
@@ -460,198 +679,6 @@
     for part in range(2):
         for side in range(2):
             edges[part, side].wait_send()
-
-
-def analysis_kernel(
-    x_ref,
-    slots_ref,
-    tab_ref,
-    row_ref,
-    count_ref,
-    out_ref,
-    state_ref,
-    part_ref,
-    anom_ref,
-    scaled_ref,
-    innov_ref,
-    lhs_ref,
-    weight_ref,
-    dev_ref,
-    out_sem,
-):
-    gx = lax.axis_index("gx")
-    gy = lax.axis_index("gy")
-    per_square = 1.0 / count_ref[3:4, :]
-    lane = iota((BLOCK, 128), 1)
-    member = lane < M
-    counts = [jnp.max(count_ref[i : i + 1, :]).astype(jnp.int32) for i in range(3)]
-    blocks0, blocks0_wide, blocks1 = [(n + BLOCK - 1) // BLOCK for n in counts]
-    for i, piece in enumerate(split3(slots_ref[...])):
-        part_ref[i] = piece
-    ocean = count_ref[4:8, :]
-    exact = functools.partial(
-        lax.dot_general, precision=lax.Precision.HIGHEST, preferred_element_type=F32
-    )
-
-    def near_x(gap):
-        gap = jnp.where(gap >= NX / 2, gap - NX, gap)
-        return jnp.where(gap < -NX / 2, gap + NX, gap)
-
-    def load(b, j):
-        start = pl.multiple_of(j * BLOCK, BLOCK)
-        tab = tab_ref[b, pl.ds(start, BLOCK), :]
-        slot = tab[:, M + 4 : M + 5]
-        hot = jnp.where(iota((BLOCK, SLOTS), 1).astype(F32) == slot, 1.0, 0.0).astype(BF16)
-        prior = dot(hot, part_ref[0]) + dot(hot, part_ref[1]) + dot(hot, part_ref[2])
-        if b:
-            prior = pltpu.roll(prior, 64, 1)
-        return tab, prior
-
-    def finish(b, j, tab, prior):
-        prior = jnp.where(member, prior, 0.0)
-        anomaly = jnp.where(
-            member, prior - jnp.sum(prior, axis=1, keepdims=True) * (1.0 / M), 0.0
-        )
-        spread = jnp.sum(anomaly * anomaly, axis=1, keepdims=True) * (1.0 / (M - 1))
-        filled = tab[:, M + 5 : M + 6]
-        scale = filled / ((M - 1) * (spread + tab[:, M + 1 : M + 2] + (1.0 - filled)))
-        innovation = jnp.where(member, tab, 0.0) - prior
-        if b == 0:
-            scaled_ref[j] = anomaly * scale
-            innov_ref[j] = innovation
-        high = anomaly.astype(BF16).astype(F32)
-        lhs = high + pltpu.roll(high, M, 1) + pltpu.roll(anomaly - high, 2 * M, 1)
-        anom_ref[b, j] = lhs.astype(BF16)
-        turned = innovation.T[0:M, :]
-        high = turned.astype(BF16).astype(F32)
-        lhs = jnp.concatenate(
-            [
-                jnp.concatenate([high, high], axis=1),
-                jnp.concatenate([turned - high, jnp.zeros_like(high)], axis=1),
-            ],
-            axis=0,
-        )
-        lhs_ref[b, j] = lhs.astype(BF16)
-        gap = near_x(tab[:, M + 3 : M + 4] - (gx * COLS + lane).astype(F32))
-        square = gap * gap
-        for r in range(ROWS):
-            gap = tab[:, M + 2 : M + 3] - (gy * ROWS + r).astype(F32)
-            taper = jnp.maximum(0.0, 1.0 - (square + gap * gap) * per_square)
-            weight_ref[b, j, :, 128 * r : 128 * r + 128] = taper * scale
-
-    def first_batch(j, carry):
-        tab, prior = load(0, j)
-        finish(0, j, tab, prior)
-        return carry
-
-    first_batch(0, 0)
-    lax.fori_loop(1, blocks0_wide, first_batch, 0)
-
-    def deviation_of(prior):
-        inside = jnp.where(member, prior, 0.0)
-        mean = jnp.sum(inside, axis=1, keepdims=True) * (1.0 / M)
-        return inside, jnp.where(member, inside - mean, 0.0)
-
-    def effect(i, tab, deviation):
-        cover = exact(deviation, scaled_ref[i], (((1,), (1,)), ((), ())))
-        window = pl.ds(pl.multiple_of(i * BLOCK, BLOCK), BLOCK)
-        gap_x = near_x(row_ref[0, 3:4, window] - tab[:, M + 3 : M + 4])
-        gap_y = row_ref[0, 2:3, window] - tab[:, M + 2 : M + 3]
-        taper = jnp.maximum(0.0, 1.0 - (gap_x * gap_x + gap_y * gap_y) * per_square)
-        return exact(cover * taper, innov_ref[i], (((1,), (0,)), ((), ())))
-
-    def second_batch(j, carry):
-        tab, prior = load(1, j)
-        inside, deviation = deviation_of(prior)
-        total = lax.fori_loop(
-            1,
-            blocks0_wide,
-            lambda i, total: total + effect(i, tab, deviation),
-            effect(0, tab, deviation),
-        )
-        finish(1, j, tab, inside + prior[:, M : M + 1] * total)
-        return carry
-
-    def spread_field(b, source, f):
-        for r in range(ROWS):
-            x = source[f * ROWS + r]
-            deviation = x - jnp.sum(x, axis=0, keepdims=True) * (1.0 / M)
-            high = deviation.astype(BF16).astype(F32)
-            stack = jnp.concatenate(
-                [high, deviation - high, high, jnp.zeros((8, 128), F32)], axis=0
-            )
-            dev_ref[b, f, :, 128 * r : 128 * r + 128] = stack.astype(BF16)
-
-    def increment(b, j, f):
-        cover = dot(anom_ref[b, j], dev_ref[b, f])
-        gain = cover * weight_ref[b, j]
-        high = gain.astype(BF16)
-        low = (gain - high.astype(F32)).astype(BF16)
-        both = dot(lhs_ref[b, j], jnp.concatenate([high, low], axis=0))
-        return both[0:M] + both[M : 2 * M]
-
-    def apply_field(b, source, f):
-        spread_field(b, source, f)
-        change = increment(b, 0, f)
-        for r in range(ROWS):
-            state_ref[f * ROWS + r] = (
-                source[f * ROWS + r] + ocean[r : r + 1, :] * change[:, 128 * r : 128 * r + 128]
-            )
-
-    def store(f):
-        for r in range(ROWS):
-            i = f * ROWS + r
-            pltpu.make_async_copy(state_ref.at[i], out_ref.at[:, i, 0, :], out_sem.at[i]).start()
-
-    short = (blocks0 <= 1) & (blocks1 <= 1)
-
-    @pl.when(short)
-    def _():
-        tab, prior = load(1, 0)
-        inside, deviation = deviation_of(prior)
-        extra = lax.fori_loop(
-            1,
-            blocks0_wide,
-            lambda i, total: total + effect(i, tab, deviation),
-            jnp.zeros((BLOCK, 128), F32),
-        )
-        total = extra + effect(0, tab, deviation)
-        finish(1, 0, tab, inside + prior[:, M : M + 1] * total)
-        for f in range(FIELDS):
-            apply_field(0, x_ref, f)
-        for f in range(FIELDS):
-            apply_field(1, state_ref, f)
-            store(f)
-
-    @pl.when(jnp.logical_not(short))
-    def _():
-        second_batch(0, 0)
-        lax.fori_loop(1, blocks1, second_batch, 0)
-        for b, blocks, source in ((0, blocks0, x_ref), (1, blocks1, state_ref)):
-
-            def field(f, carry, b=b, source=source):
-                apply_field(b, source, f)
-                return carry
-
-            lax.fori_loop(0, FIELDS, field, 0)
-
-            def more(j, carry, b=b):
-                def field_more(f, inner_carry):
-                    change = increment(b, j, f)
-                    for r in range(ROWS):
-                        state_ref[f * ROWS + r] += (
-                            ocean[r : r + 1, :] * change[:, 128 * r : 128 * r + 128]
-                        )
-                    return inner_carry
-
-                return lax.fori_loop(0, FIELDS, field_more, carry)
-
-            lax.fori_loop(1, blocks, more, 0)
-        for f in range(FIELDS):
-            store(f)
-
-    for i in range(FIELDS * ROWS):
-        pltpu.make_async_copy(state_ref.at[i], out_ref.at[:, i, 0, :], out_sem.at[i]).wait()
 
 
 def local(
@@ -672,9 +699,11 @@
     hbm = pl.BlockSpec(memory_space=pltpu.HBM)
     shape = jax.ShapeDtypeStruct
     dma = pltpu.SemaphoreType.DMA
-    x, slots, tab, rows, count = pl.pallas_call(
+    most = SLOTS // BLOCK
+    done, x, slots, tab, rows, count = pl.pallas_call(
         forecast_kernel,
         out_shape=(
+            shape((FIELDS * ROWS, M, COLS), F32),
             shape((FIELDS * ROWS, M, COLS), F32),
             shape((SLOTS, 128), F32),
             shape((2, SLOTS, 128), F32),
@@ -682,7 +711,7 @@
             shape((8, 128), F32),
         ),
         in_specs=[hbm] * 11 + [pl.BlockSpec(memory_space=pltpu.SMEM)],
-        out_specs=(vmem,) * 5,
+        out_specs=(vmem,) * 6,
         scratch_shapes=[
             pltpu.VMEM((FIELDS, ROWS, M, COLS), F32),
             pltpu.VMEM((FIELDS, 2, 2, M, COLS), F32),
@@ -706,6 +735,13 @@
             pltpu.VMEM((2, NOBS), F32),
             pltpu.VMEM((2, NOBS), F32),
             pltpu.VMEM((2, M, NOBS), F32),
+            pltpu.VMEM((3, SLOTS, 128), BF16),
+            pltpu.VMEM((2, 1, BLOCK, 128), BF16),
+            pltpu.VMEM((WIDE, BLOCK, 128), F32),
+            pltpu.VMEM((WIDE, BLOCK, 128), F32),
+            pltpu.VMEM((2, 1, 2 * M, 2 * BLOCK), BF16),
+            pltpu.VMEM((2, 1, BLOCK, ROWS * COLS), F32),
+            pltpu.VMEM((2, FIELDS, 128, ROWS * COLS), BF16),
             dma((10,)),
             dma((FIELDS, ROWS)),
             dma((FIELDS, 2)),
@@ -739,14 +775,12 @@
         ),
         radius,
     )
-    most = SLOTS // BLOCK
     out = pl.pallas_call(
         analysis_kernel,
         out_shape=shape((M, FIELDS * ROWS, 1, COLS), F32),
-        in_specs=[vmem] * 5,
+        in_specs=[vmem] * 6,
         out_specs=hbm,
         scratch_shapes=[
-            pltpu.VMEM((FIELDS * ROWS, M, COLS), F32),
             pltpu.VMEM((3, SLOTS, 128), BF16),
             pltpu.VMEM((2, most, BLOCK, 128), BF16),
             pltpu.VMEM((most, BLOCK, 128), F32),
@@ -754,10 +788,11 @@
             pltpu.VMEM((2, most, 2 * M, 2 * BLOCK), BF16),
             pltpu.VMEM((2, most, BLOCK, ROWS * COLS), F32),
             pltpu.VMEM((2, FIELDS, 128, ROWS * COLS), BF16),
+            pltpu.VMEM((FIELDS * ROWS, M, COLS), F32),
             dma((FIELDS * ROWS,)),
         ],
         compiler_params=pltpu.CompilerParams(vmem_limit_bytes=40 << 20),
-    )(x, slots, tab, rows, count)
+    )(done, x, slots, tab, rows, count)
     return out.reshape(ensemble.shape)
 
 

time: 42.8 us -> 40.1 us (0.937)
  Pallas kernels: 42 us -> 39 us
    pallas_call x1, Pallas kernels: 5.7 us -> 1.09 us  [local(): pl.pallas_call(analysis_kernel, out_shape=shape((M, FIELDS * ROWS, 1, COL...]
    pallas_call x1, Pallas kernels: 36.3 us -> 37.9 us  [local(): pl.pallas_call(forecast_kernel, out_shape=(shape((FIELDS * ROWS, M, COLS)...]
where the time goes in v3:
time: 40.1 us; the launch traced here: 39.7 us
  Pallas kernels  39 us (97%)
  between operations  0.66 us (2%)
    pallas_call x1, Pallas kernels, local(): pl.pallas_call(forecast_kernel, out_shape=(shape((FIELDS * ROWS, M, COLS)...  37.9 us
    pallas_call x1, Pallas kernels, local(): pl.pallas_call(analysis_kernel, out_shape=shape((M, FIELDS * ROWS, 1, COL...  1.09 us

profile of v3, /device:TPU:1, one launch (start us, length us, event | category | flops | bytes accessed | tf_op | source)
XLA Modules:
  0.0 39.7 jit_solution(13582889529620800596)
XLA Ops:
  0.7 37.9 %shard_map.118 = (f32[32,40,128]{2,1,0:T(8,128)S(1)}, f32[32,40,128]{2,1,0:T(8,128)S(1)}, f32[384,128]{1,0:T(8,128)S(1)}, f32[2,384,128]{2,1,0:T(8,128)S(1)}, f3...) custom-call(f32[40,32,1,128]{3,2,1,0:T(1,128)} %bitcast.6, f32[8,128]{1,0:T(8,128)} %bitcast.8, f32[8,128]{1,0:T(8,128)} %bitcast.9, ...), custom_call_target="tpu_custom_call" | custom-call | tf_op jit(solution)/shard_map/pallas_call | solution.py:703
  38.6 1.1 %shard_map.119 = f32[40,32,1,128]{3,2,1,0:T(1,128)} custom-call(f32[32,40,128]{2,1,0:T(8,128)S(1)} %get-tuple-element.11.done_ref, f32[32,40,128]{2,1,0:T(8,128)S(1)} %get-tuple-element.12.x_ref, f32[384,128]{1,0:T(8,128)S(1)} %get-tuple-element.13.slots_ref, f32[2,384,128]{2,1,0:T(8,128)S(1)} %get-tuple-element.14.tab_ref, ...), custom_call_target="tpu_custom_call" | custom-call | tf_op jit(solution)/shard_map/pallas_call | solution.py:778

commit v4 on v3

--- a/solution.py
+++ b/solution.py
@@ -651,12 +651,12 @@
         part_ref[i] = piece
     for j in range(WIDE):
         a.finish(0, j, *a.load(0, j), grid=j == 0)
+    for f in ORDER[:EARLY]:
+        a.apply_field(0, x_ref, f)
     tab, prior = a.load(1, 0)
     inside, deviation = a.deviation_of(prior)
     total = sum(a.effect(j, tab, deviation) for j in range(WIDE))
     a.finish(1, 0, tab, inside + prior[:, M : M + 1] * total)
-    for f in ORDER[:EARLY]:
-        a.apply_field(0, x_ref, f)
     for f in ORDER[:EARLY]:
         a.spread_field(1, done_ref, f)
         a.apply_field(1, done_ref, f)

time: 40.1 us -> 40.9 us (1.020)
  the two profiles are of different devices: /device:TPU:1 before, /device:TPU:217 now
where the time goes in v4:
time: 40.9 us; the launch traced here: 40.8 us
  Pallas kernels  40.1 us (98%)
  between operations  0.66 us (2%)
    pallas_call x1, Pallas kernels, local(): pl.pallas_call(forecast_kernel, out_shape=(shape((FIELDS * ROWS, M, COLS)...  39 us
    pallas_call x1, Pallas kernels, local(): pl.pallas_call(analysis_kernel, out_shape=shape((M, FIELDS * ROWS, 1, COL...  1.09 us

profile of v4, /device:TPU:217, one launch (start us, length us, event | category | flops | bytes accessed | tf_op | source)
XLA Modules:
  0.0 40.8 jit_solution(6100005327142970704)
XLA Ops:
  0.7 39.0 %shard_map.118 = (f32[32,40,128]{2,1,0:T(8,128)S(1)}, f32[32,40,128]{2,1,0:T(8,128)S(1)}, f32[384,128]{1,0:T(8,128)S(1)}, f32[2,384,128]{2,1,0:T(8,128)S(1)}, f3...) custom-call(f32[40,32,1,128]{3,2,1,0:T(1,128)} %bitcast.6, f32[8,128]{1,0:T(8,128)} %bitcast.8, f32[8,128]{1,0:T(8,128)} %bitcast.9, ...), custom_call_target="tpu_custom_call" | custom-call | tf_op jit(solution)/shard_map/pallas_call | solution.py:703
  39.7 1.1 %shard_map.119 = f32[40,32,1,128]{3,2,1,0:T(1,128)} custom-call(f32[32,40,128]{2,1,0:T(8,128)S(1)} %get-tuple-element.11.done_ref, f32[32,40,128]{2,1,0:T(8,128)S(1)} %get-tuple-element.12.x_ref, f32[384,128]{1,0:T(8,128)S(1)} %get-tuple-element.13.slots_ref, f32[2,384,128]{2,1,0:T(8,128)S(1)} %get-tuple-element.14.tab_ref, ...), custom_call_target="tpu_custom_call" | custom-call | tf_op jit(solution)/shard_map/pallas_call | solution.py:778
